TPU v7x, 32 devices: a whole 2x2x4 slice. The times are simulated.
32 devices in a mesh: ctx: 16 (over z, x, core), fsdp: 2 (over y).
Axes of the slice: x: 2, y: 2, z: 4, core: 2. Of those that a mesh axis runs over, the one named last changes fastest.
Arguments:
- inputs: bfloat16 [2, 2048, 1280], P('fsdp', 'ctx'), may hold values from -6 to 6
- norm1_gain: bfloat16 [1280], P('fsdp'), may hold values from 0.099609375 to 1.8984375
- w_query: bfloat16 [1280, 1280], P('fsdp'), may hold values from -0.15625 to 0.15625
- w_key: bfloat16 [1280, 1280], P('fsdp'), may hold values from -0.15625 to 0.15625
- w_value: bfloat16 [1280, 1280], P('fsdp'), may hold values from -0.15625 to 0.15625
- w_output: bfloat16 [1280, 1280], P('fsdp'), may hold values from -0.625 to 0.625
- norm2_gain: bfloat16 [1280], P('fsdp'), may hold values from 0.099609375 to 1.8984375
- router: bfloat16 [1280, 16], P('fsdp'), may hold values from -0.083984375 to 0.083984375
- shared_gate_up_weight: bfloat16 [1280, 1792], P('fsdp'), may hold values from -0.15625 to 0.15625
- shared_down_weight: bfloat16 [896, 1280], P('fsdp'), may hold values from -0.1875 to 0.1875
- expert_in: bfloat16 [16, 1280, 1792], P('ctx', 'fsdp'), may hold values from -0.15625 to 0.15625
- expert_out: bfloat16 [16, 896, 1280], P('ctx', 'fsdp'), may hold values from -0.1875 to 0.1875
- picks: int32 [2, 2048, 7], P('fsdp', 'ctx'), may hold values from 0 to 15, all different within a row
- fill_order: int32 [2, 16, 896], P('fsdp', 'ctx'), may hold values from 0 to 895, each once within a row
- grad_out: bfloat16 [2, 2048, 1280], P('fsdp', 'ctx'), may hold values from -6 to 6
Outputs:
- layer_out: bfloat16 [2, 2048, 1280], P('fsdp', 'ctx')
- grad_inputs: float32 [2, 2048, 1280], P('fsdp', 'ctx')
- grad_norm1: float32 [1280], P('fsdp')
- grad_query: float32 [1280, 1280], P('fsdp')
- grad_key: float32 [1280, 1280], P('fsdp')
- grad_value: float32 [1280, 1280], P('fsdp')
- grad_output: float32 [1280, 1280], P('fsdp')
- grad_norm2: float32 [1280], P('fsdp')
- grad_router: float32 [1280, 16], P('fsdp')
- grad_shared_in: float32 [1280, 1792], P('fsdp')
- grad_shared_out: float32 [896, 1280], P('fsdp')
- grad_expert_in: float32 [16, 1280, 1792], P('ctx', 'fsdp')
- grad_expert_out: float32 [16, 896, 1280], P('ctx', 'fsdp')
Inputs may be any that keep to these rules, and one draw needn't show every extreme that they name: Each token's 7 picks name different experts, and every expert is picked by some token. `fill_order`: for each sequence and run c, the 896 entries are a permutation; entry t * 7 + k belongs to token c * 128 + t and its k-th pick.
All inputs are finite; a program needn't handle non-finite values.
Results may differ from a plain program's by a relative error of at most 0.018.
Values may be sent and summed in bfloat16 or wider, within the bound.
No kernel may reach another device: no remote copies, remote signals or barrier semaphores. Data moves between devices by JAX's collectives and lax.ppermute only.
A program may use at most 320 MiB of HBM per device.

v0:
```python
import math

import jax
import jax.numpy as jnp
from jax import lax
from jax.sharding import PartitionSpec as P

HEADS = 10
HEAD_DIM = 128
EXP_HID = 896
TOP = 7
BLOCK = 256
TOK_DEV = 128


epsilon = 1e-06
masked_score = -1000000000.0
start_peak = -1e30
top_score_value = lax.Precision.HIGHEST


def rms_scale(values):
    return lax.rsqrt(jnp.mean(values * values, axis=-1, keepdims=True) + epsilon)


def rotary_tables(positions, width):
    half = width // 2
    freqs = jnp.exp(-math.log(10000.0) * jnp.arange(half, dtype=jnp.float32) * 2.0 / width)
    angles = positions.astype(jnp.float32)[:, None] * freqs[None, :]
    cosine = jnp.concatenate([jnp.cos(angles), jnp.cos(angles)], axis=-1)
    sine = jnp.concatenate([jnp.sin(angles), jnp.sin(angles)], axis=-1)
    return (cosine, sine)


def rotate(values, cosine, sine):
    half = values.shape[-1] // 2
    turned = jnp.concatenate([-values[..., half:], values[..., :half]], axis=-1)
    return values * cosine[:, None, :] + turned * sine[:, None, :]


def rotate_back(grads, cosine, sine):
    half = grads.shape[-1] // 2
    scaled = grads * sine[:, None, :]
    return grads * cosine[:, None, :] + jnp.concatenate(
        [scaled[..., half:], -scaled[..., :half]], axis=-1
    )


def slot_plan(span_picks, span_order, experts, capacity):
    top_count = span_picks.shape[-1]
    chosen = span_picks.reshape(-1)
    pairs = chosen.shape[0]
    sequence = jnp.argsort(span_order)
    ordered = chosen[sequence]
    onehot = (ordered[:, None] == jnp.arange(experts, dtype=jnp.int32)[None, :]).astype(jnp.int32)
    before = jnp.cumsum(onehot, axis=0) - onehot
    slots = jnp.sum(before * onehot, axis=1)[span_order]
    kept = slots < capacity
    target = jnp.where(kept, chosen * capacity + slots, experts * capacity)
    pair_ids = jnp.arange(pairs, dtype=jnp.int32)
    pair_of_slot = jnp.zeros((experts * capacity,), jnp.int32).at[target].set(pair_ids, mode="drop")
    filled = jnp.zeros((experts * capacity,), jnp.int32).at[target].set(1, mode="drop")
    return (target, kept, pair_of_slot // top_count, pair_of_slot, filled)


def over_shards(step, carry, piece):
    parts = jax.tree.map(lambda array: array.reshape((-1, TOK_DEV) + array.shape[1:]), piece)
    count = jax.tree.leaves(parts)[0].shape[0]

    def visit(state, item):
        shard, number = item
        return (step(state, shard, number * TOK_DEV), None)

    result, _ = lax.scan(visit, carry, (parts, jnp.arange(count, dtype=jnp.int32)))
    return result


def norm_back(grad_normed, values, scale_rows, gain):
    grad_gain = jnp.sum(grad_normed * values * scale_rows, axis=0)
    grad_hat = grad_normed * gain
    cubed = scale_rows * scale_rows * scale_rows
    grad_in = scale_rows * grad_hat - values * cubed * jnp.mean(
        grad_hat * values, axis=-1, keepdims=True
    )
    return (grad_gain, grad_in)


def swiglu_back(grad_hidden, projected):
    gate_part = projected[..., :EXP_HID]
    up_part = projected[..., EXP_HID:]
    sigmoid = jax.nn.sigmoid(gate_part)
    grad_gate = grad_hidden * up_part * sigmoid * (1.0 + gate_part * (1.0 - sigmoid))
    grad_up = grad_hidden * jax.nn.silu(gate_part)
    return jnp.concatenate([grad_gate, grad_up], axis=-1).astype(jnp.bfloat16)


def on_device(
    inputs,
    norm1_gain,
    w_query,
    w_key,
    w_value,
    w_output,
    norm2_gain,
    router,
    shared_gate_up_weight,
    shared_down_weight,
    expert_in,
    expert_out,
    picks,
    fill_order,
    grad_out,
):
    gathered = (
        lax.all_gather(norm1_gain, "fsdp", axis=0, tiled=True),
        lax.all_gather(w_query, "fsdp", axis=0, tiled=True),
        lax.all_gather(w_key, "fsdp", axis=0, tiled=True),
        lax.all_gather(w_value, "fsdp", axis=0, tiled=True),
        lax.all_gather(w_output, "fsdp", axis=0, tiled=True),
        lax.all_gather(norm2_gain, "fsdp", axis=0, tiled=True),
        lax.all_gather(router, "fsdp", axis=0, tiled=True),
        lax.all_gather(shared_gate_up_weight, "fsdp", axis=0, tiled=True),
        lax.all_gather(shared_down_weight, "fsdp", axis=0, tiled=True),
    )
    gain_one, query_w, key_w, value_w, output_w, gain_two, router_w, shared_in_w, shared_out_w = (
        gathered
    )
    gain_one = gain_one.astype(jnp.float32)
    gain_two = gain_two.astype(jnp.float32)
    tokens = inputs.shape[1]
    width = inputs.shape[2]
    score_scale = 1.0 / math.sqrt(HEAD_DIM)
    offset = lax.axis_index("ctx") * tokens
    positions = offset + jnp.arange(tokens, dtype=jnp.int32)
    cosine, sine = rotary_tables(positions, HEAD_DIM)
    last_key = ((offset + tokens - 1) // BLOCK + 1) * BLOCK - 1
    first_query = offset // BLOCK * BLOCK
    resid = inputs[0].astype(jnp.float32)
    scale_one = rms_scale(resid)
    normed1 = (resid * scale_one * gain_one).astype(jnp.bfloat16)
    query_proj = jnp.dot(normed1, query_w, preferred_element_type=jnp.float32).reshape(
        tokens, HEADS, HEAD_DIM
    )
    key_proj = jnp.dot(normed1, key_w, preferred_element_type=jnp.float32).reshape(
        tokens, HEADS, HEAD_DIM
    )
    query_rows = rotate(query_proj, cosine, sine).astype(jnp.bfloat16)
    key_rows = rotate(key_proj, cosine, sine).astype(jnp.bfloat16)
    value_rows = (
        jnp.dot(normed1, value_w, preferred_element_type=jnp.float32)
        .astype(jnp.bfloat16)
        .reshape(tokens, HEADS, HEAD_DIM)
    )

    def shard_weights(query_part, key_part, query_pos, key_pos):
        raw = jnp.einsum("qhd,khd->qhk", query_part, key_part, preferred_element_type=jnp.float32)
        allowed = (key_pos // BLOCK)[None, None, :] <= (query_pos // BLOCK)[:, None, None]
        scores = jnp.where(allowed, raw * score_scale, masked_score)
        peak = jnp.max(scores, axis=-1)
        return (peak, jnp.exp(scores - peak[..., None]))

    def forward_step(state, key_start, produce):

        def forward_compute(current):
            peak_run, total_run, numer_run = current
            key_part, value_part = produce()
            key_pos = key_start + jnp.arange(key_part.shape[0], dtype=jnp.int32)
            peak, weights = shard_weights(query_rows, key_part, positions, key_pos)
            partial_value = jnp.einsum(
                "qhk,khd->qhd",
                weights.astype(jnp.bfloat16),
                value_part,
                preferred_element_type=jnp.float32,
            )
            new_peak = jnp.maximum(peak_run, peak)
            keep = jnp.exp(peak_run - new_peak)
            factor = jnp.exp(peak - new_peak)
            return (
                new_peak,
                total_run * keep + factor * jnp.sum(weights, axis=-1),
                numer_run * keep[..., None] + factor[..., None] * partial_value,
            )

        return lax.cond(key_start > last_key, lambda current: current, forward_compute, state)

    initial = (
        jnp.full((tokens, HEADS), start_peak, jnp.float32),
        jnp.zeros((tokens, HEADS), jnp.float32),
        jnp.zeros((tokens, HEADS, HEAD_DIM), jnp.float32),
    )

    def from_pairs(state, shard, key_start):
        return forward_step(
            state,
            key_start,
            lambda: (shard[0].reshape(-1, HEADS, HEAD_DIM), shard[1].reshape(-1, HEADS, HEAD_DIM)),
        )

    state = over_shards(
        from_pairs,
        initial,
        (
            lax.all_gather(key_rows.reshape(tokens, width), "ctx", axis=0, tiled=True),
            lax.all_gather(value_rows.reshape(tokens, width), "ctx", axis=0, tiled=True),
        ),
    )
    peak_final, total_final, numer_final = state
    context = numer_final / total_final[..., None]
    log_total = peak_final + jnp.log(total_final)
    attended = context.reshape(tokens, width).astype(jnp.bfloat16)
    second = resid + jnp.dot(attended, output_w, preferred_element_type=jnp.float32)
    scale_two = rms_scale(second)
    second_normalized = (second * scale_two * gain_two).astype(jnp.bfloat16)
    router_scores = jnp.dot(second_normalized, router_w, preferred_element_type=jnp.float32)
    experts = router_w.shape[1]
    chosen = picks[0]
    onehot = (chosen[:, :, None] == jnp.arange(experts, dtype=jnp.int32)[None, None, :]).astype(
        jnp.float32
    )
    selected = jnp.einsum("tke,te->tk", onehot, router_scores, precision=top_score_value)
    gates = jax.nn.softmax(selected, axis=-1)
    shared_expert_projected = jnp.dot(
        second_normalized, shared_in_w, preferred_element_type=jnp.float32
    )
    shared_expert_hidden = (
        jax.nn.silu(shared_expert_projected[:, :EXP_HID]) * shared_expert_projected[:, EXP_HID:]
    ).astype(jnp.bfloat16)
    shared_expert_output = jnp.dot(
        shared_expert_hidden, shared_out_w, preferred_element_type=jnp.float32
    )
    capacity = tokens * TOP // experts
    target, kept, token_of_slot, pair_of_slot, filled = slot_plan(
        chosen, fill_order[0, 0], experts, capacity
    )
    send = jnp.where(
        filled[:, None] > 0, second_normalized[token_of_slot], jnp.zeros((), jnp.bfloat16)
    ).reshape(experts, capacity, width)
    expert_in_w, expert_out_w = (
        lax.all_gather(expert_in, "fsdp", axis=1, tiled=True),
        lax.all_gather(expert_out, "fsdp", axis=1, tiled=True),
    )
    local = expert_in_w.shape[0]
    sources = lax.axis_size("ctx")
    received = lax.all_to_all(send, "ctx", split_axis=0, concat_axis=0, tiled=True)
    grouped = received.reshape(sources, local, -1, width)
    projected = jnp.einsum(
        "sxcd,xdf->sxcf", grouped, expert_in_w, preferred_element_type=jnp.float32
    )
    hidden = (jax.nn.silu(projected[..., :EXP_HID]) * projected[..., EXP_HID:]).astype(jnp.bfloat16)
    produced = (
        jnp.einsum("sxcf,xfd->sxcd", hidden, expert_out_w, preferred_element_type=jnp.float32)
        .astype(jnp.bfloat16)
        .reshape(received.shape)
    )
    returned = lax.all_to_all(produced, "ctx", split_axis=0, concat_axis=0, tiled=True)
    extra = ()
    results = (returned, received) + extra
    returned = results[0]
    received = results[1]
    slot_count = experts * capacity
    clipped = jnp.minimum(target, slot_count - 1)
    chosen_experts = (
        returned.reshape(slot_count, width)[clipped].reshape(tokens, TOP, width).astype(jnp.float32)
    )
    kept_f = kept.reshape(tokens, TOP).astype(jnp.float32)
    token_expert_weight = gates * kept_f
    routed_output = jnp.einsum(
        "tk,tkd->td", token_expert_weight, chosen_experts, precision=top_score_value
    )
    layer_out = (second + shared_expert_output + routed_output).astype(jnp.bfloat16)
    grad_low = grad_out[0]
    grad_f = grad_low.astype(jnp.float32)
    grad_pair = jnp.einsum("td,tkd->tk", grad_f, chosen_experts, precision=top_score_value) * kept_f
    slot_weight = token_expert_weight.reshape(-1)[pair_of_slot] * filled.astype(jnp.float32)
    grad_back = (
        (grad_f[token_of_slot] * slot_weight[:, None])
        .astype(jnp.bfloat16)
        .reshape(experts, capacity, width)
    )
    grad_received = lax.all_to_all(grad_back, "ctx", split_axis=0, concat_axis=0, tiled=True)
    grouped = received.reshape(sources, local, -1, width)
    grad_grouped = grad_received.reshape(sources, local, -1, width)
    projected = jnp.einsum(
        "sxcd,xdf->sxcf", grouped, expert_in_w, preferred_element_type=jnp.float32
    )
    hidden = (jax.nn.silu(projected[..., :EXP_HID]) * projected[..., EXP_HID:]).astype(jnp.bfloat16)
    grad_hidden = jnp.einsum(
        "sxcd,xfd->sxcf", grad_grouped, expert_out_w, preferred_element_type=jnp.float32
    )
    grad_expert_out = jnp.einsum(
        "sxcf,sxcd->xfd", hidden, grad_grouped, preferred_element_type=jnp.float32
    )
    grad_projected = swiglu_back(grad_hidden, projected)
    grad_expert_in = jnp.einsum(
        "sxcd,sxcf->xdf", grouped, grad_projected, preferred_element_type=jnp.float32
    )
    grad_rows_in = (
        jnp.einsum(
            "sxcf,xdf->sxcd", grad_projected, expert_in_w, preferred_element_type=jnp.float32
        )
        .astype(jnp.bfloat16)
        .reshape(received.shape)
    )
    grad_returned = lax.all_to_all(grad_rows_in, "ctx", split_axis=0, concat_axis=0, tiled=True)
    expert_sums = (
        lax.psum_scatter(
            grad_expert_in.astype(jnp.bfloat16), "fsdp", scatter_dimension=1, tiled=True
        ).astype(jnp.float32),
        lax.psum_scatter(
            grad_expert_out.astype(jnp.bfloat16), "fsdp", scatter_dimension=1, tiled=True
        ).astype(jnp.float32),
    )
    grad_routed = (
        grad_returned.reshape(slot_count, width)[clipped]
        .reshape(tokens, TOP, width)
        .astype(jnp.float32)
    )
    grad_routed = jnp.sum(grad_routed * kept_f[..., None], axis=1)
    grad_sel = gates * (grad_pair - jnp.sum(gates * grad_pair, axis=-1, keepdims=True))
    grad_logits = jnp.einsum("tk,tke->te", grad_sel, onehot, precision=top_score_value).astype(
        jnp.bfloat16
    )
    grad_router = jnp.dot(second_normalized.T, grad_logits, preferred_element_type=jnp.float32)
    grad_shidden = jnp.dot(grad_low, shared_out_w.T, preferred_element_type=jnp.float32)
    grad_shared_out = jnp.dot(shared_expert_hidden.T, grad_low, preferred_element_type=jnp.float32)
    grad_sproj = swiglu_back(grad_shidden, shared_expert_projected)
    grad_shared_in = jnp.dot(second_normalized.T, grad_sproj, preferred_element_type=jnp.float32)
    grad_normed2 = (
        grad_routed
        + jnp.dot(grad_sproj, shared_in_w.T, preferred_element_type=jnp.float32)
        + jnp.dot(grad_logits, router_w.T, preferred_element_type=jnp.float32)
    )
    grad_gain_two, grad_from_norm = norm_back(grad_normed2, second, scale_two, gain_two)
    grad_second = grad_f + grad_from_norm
    grad_mixed = grad_second.astype(jnp.bfloat16)
    grad_output_w = jnp.dot(attended.T, grad_mixed, preferred_element_type=jnp.float32)
    grad_context = jnp.dot(grad_mixed, output_w.T, preferred_element_type=jnp.float32).astype(
        jnp.bfloat16
    )
    grad_context_f = grad_context.astype(jnp.float32).reshape(tokens, HEADS, HEAD_DIM)
    delta = jnp.sum(grad_context_f * context, axis=-1)
    log_all, delta_all = (
        lax.all_gather(log_total, "ctx", axis=0, tiled=True),
        lax.all_gather(delta, "ctx", axis=0, tiled=True),
    )

    def query_step(accum, shard, key_start):

        def query_compute(current):
            key_part = shard[0].reshape(-1, HEADS, HEAD_DIM)
            value_part = shard[1].reshape(-1, HEADS, HEAD_DIM)
            key_pos = key_start + jnp.arange(key_part.shape[0], dtype=jnp.int32)
            peak, weights = shard_weights(query_rows, key_part, positions, key_pos)
            factor = jnp.exp(peak - log_total)
            grad_part = (grad_context_f * factor[..., None]).astype(jnp.bfloat16)
            grad_weights = jnp.einsum(
                "qhd,khd->qhk", grad_part, value_part, preferred_element_type=jnp.float32
            )
            grad_scores = weights * (grad_weights - (factor * delta)[..., None])
            grad_raw = (grad_scores * score_scale).astype(jnp.bfloat16)
            return current + jnp.einsum(
                "qhk,khd->qhd", grad_raw, key_part, preferred_element_type=jnp.float32
            )

        return lax.cond(key_start > last_key, lambda current: current, query_compute, accum)

    grad_queries = over_shards(
        query_step,
        jnp.zeros((tokens, HEADS, HEAD_DIM), jnp.float32),
        (
            lax.all_gather(key_rows.reshape(tokens, width), "ctx", axis=0, tiled=True),
            lax.all_gather(value_rows.reshape(tokens, width), "ctx", axis=0, tiled=True),
        ),
    )

    def key_step(accum, shard, query_start):

        def key_compute(current):
            grad_key_acc, grad_value_acc = current
            query_part = shard[0].reshape(-1, HEADS, HEAD_DIM)
            grad_ctx_part = shard[1].reshape(-1, HEADS, HEAD_DIM)
            count = query_part.shape[0]
            query_pos = query_start + jnp.arange(count, dtype=jnp.int32)
            log_part = lax.dynamic_slice_in_dim(log_all, query_start, count, 0)
            delta_part = lax.dynamic_slice_in_dim(delta_all, query_start, count, 0)
            peak, weights = shard_weights(query_part, key_rows, query_pos, positions)
            factor = jnp.exp(peak - log_part)
            grad_part = (grad_ctx_part.astype(jnp.float32) * factor[..., None]).astype(jnp.bfloat16)
            grad_value_acc = grad_value_acc + jnp.einsum(
                "qhk,qhd->khd",
                weights.astype(jnp.bfloat16),
                grad_part,
                preferred_element_type=jnp.float32,
            )
            grad_weights = jnp.einsum(
                "qhd,khd->qhk", grad_part, value_rows, preferred_element_type=jnp.float32
            )
            grad_scores = weights * (grad_weights - (factor * delta_part)[..., None])
            grad_raw = (grad_scores * score_scale).astype(jnp.bfloat16)
            grad_key_acc = grad_key_acc + jnp.einsum(
                "qhk,qhd->khd", grad_raw, query_part, preferred_element_type=jnp.float32
            )
            return (grad_key_acc, grad_value_acc)

        return lax.cond(
            query_start + TOK_DEV - 1 < first_query, lambda current: current, key_compute, accum
        )

    empty_grads = (
        jnp.zeros((tokens, HEADS, HEAD_DIM), jnp.float32),
        jnp.zeros((tokens, HEADS, HEAD_DIM), jnp.float32),
    )
    grad_keys, grad_values = over_shards(
        key_step,
        empty_grads,
        (
            lax.all_gather(query_rows.reshape(tokens, width), "ctx", axis=0, tiled=True),
            lax.all_gather(grad_context, "ctx", axis=0, tiled=True),
        ),
    )
    grad_qproj = rotate_back(grad_queries, cosine, sine).reshape(tokens, width).astype(jnp.bfloat16)
    grad_kproj = rotate_back(grad_keys, cosine, sine).reshape(tokens, width).astype(jnp.bfloat16)
    grad_vproj = grad_values.reshape(tokens, width).astype(jnp.bfloat16)
    grad_query_w = jnp.dot(normed1.T, grad_qproj, preferred_element_type=jnp.float32)
    grad_key_w = jnp.dot(normed1.T, grad_kproj, preferred_element_type=jnp.float32)
    grad_value_w = jnp.dot(normed1.T, grad_vproj, preferred_element_type=jnp.float32)
    grad_normed1 = (
        jnp.dot(grad_qproj, query_w.T, preferred_element_type=jnp.float32)
        + jnp.dot(grad_kproj, key_w.T, preferred_element_type=jnp.float32)
        + jnp.dot(grad_vproj, value_w.T, preferred_element_type=jnp.float32)
    )
    grad_gain_one, grad_from_first = norm_back(grad_normed1, resid, scale_one, gain_one)
    grad_inputs = grad_second + grad_from_first
    summed = (
        lax.psum_scatter(
            grad_gain_one.astype(jnp.bfloat16), "fsdp", scatter_dimension=0, tiled=True
        ).astype(jnp.float32),
        lax.psum_scatter(
            grad_query_w.astype(jnp.bfloat16), "fsdp", scatter_dimension=0, tiled=True
        ).astype(jnp.float32),
        lax.psum_scatter(
            grad_key_w.astype(jnp.bfloat16), "fsdp", scatter_dimension=0, tiled=True
        ).astype(jnp.float32),
        lax.psum_scatter(
            grad_value_w.astype(jnp.bfloat16), "fsdp", scatter_dimension=0, tiled=True
        ).astype(jnp.float32),
        lax.psum_scatter(
            grad_output_w.astype(jnp.bfloat16), "fsdp", scatter_dimension=0, tiled=True
        ).astype(jnp.float32),
        lax.psum_scatter(
            grad_gain_two.astype(jnp.bfloat16), "fsdp", scatter_dimension=0, tiled=True
        ).astype(jnp.float32),
        lax.psum_scatter(
            grad_router.astype(jnp.bfloat16), "fsdp", scatter_dimension=0, tiled=True
        ).astype(jnp.float32),
        lax.psum_scatter(
            grad_shared_in.astype(jnp.bfloat16), "fsdp", scatter_dimension=0, tiled=True
        ).astype(jnp.float32),
        lax.psum_scatter(
            grad_shared_out.astype(jnp.bfloat16), "fsdp", scatter_dimension=0, tiled=True
        ).astype(jnp.float32),
    )
    summed = lax.psum(
        (
            summed[0],
            summed[1],
            summed[2],
            summed[3],
            summed[4],
            summed[5],
            summed[6],
            summed[7],
            summed[8],
        ),
        "ctx",
    )
    return (
        layer_out[None],
        grad_inputs[None],
        summed[0],
        summed[1],
        summed[2],
        summed[3],
        summed[4],
        summed[5],
        summed[6],
        summed[7],
        summed[8],
        expert_sums[0],
        expert_sums[1],
    )


def solution(mesh):
    placed = (
        P("fsdp", "ctx", None),
        P("fsdp"),
        P("fsdp", None),
        P("fsdp", None),
        P("fsdp", None),
        P("fsdp", None),
        P("fsdp"),
        P("fsdp", None),
        P("fsdp", None),
        P("fsdp", None),
        P("ctx", "fsdp", None),
        P("ctx", "fsdp", None),
        P("fsdp", "ctx", None),
        P("fsdp", "ctx", None),
        P("fsdp", "ctx", None),
    )
    return jax.shard_map(
        on_device,
        mesh=mesh,
        in_specs=placed,
        out_specs=(
            P("fsdp", "ctx", None),
            P("fsdp", "ctx", None),
            P("fsdp"),
            P("fsdp", None),
            P("fsdp", None),
            P("fsdp", None),
            P("fsdp", None),
            P("fsdp"),
            P("fsdp", None),
            P("fsdp", None),
            P("fsdp", None),
            P("ctx", "fsdp", None),
            P("ctx", "fsdp", None),
        ),
        check_vma=False,
    )
```

profile of v0, /device:TPU:0, one launch (start us, length us, event | category | flops | bytes accessed | tf_op | source)
XLA Modules:
  0.0 1518.2 jit_solution(8817355746859211447)
XLA Ops:
  9.5 5.3 all-gather
  15.8 42.9 %all-gather.19.cloned.1.call-done = bf16[1280,1280]{1,0:T(8,128)(2,1)} async-done(((bf16[640,1280]{1,0:T(8,128)(2,1)}), bf16[1280,1280]{1,0:T(8,128)(2,1)}) %all-gather.19.cloned.1.call-update) | async-done | bytes 3276816 | tf_op jit(solution)/shard_map/all_gather | solution.py:116
  58.7 5.6 copy.135
  64.4 42.3 %all-gather.15.cloned.1.call-done = bf16[1280,1280]{1,0:T(8,128)(2,1)} async-done(((bf16[640,1280]{1,0:T(8,128)(2,1)}), bf16[1280,1280]{1,0:T(8,128)(2,1)}) %all-gather.15.cloned.1.call-update) | async-done | bytes 3276816 | tf_op jit(solution)/shard_map/all_gather | solution.py:117
  106.7 5.6 copy.133
  112.4 3.3 fusion.106
  118.3 36.5 %all-gather.21.cloned.1.call-done = bf16[1280,1280]{1,0:T(8,128)(2,1)} async-done(((bf16[640,1280]{1,0:T(8,128)(2,1)}), bf16[1280,1280]{1,0:T(8,128)(2,1)}) %all-gather.21.cloned.1.call-update) | async-done | bytes 3276816 | tf_op jit(solution)/shard_map/all_gather | solution.py:118
  154.7 3.3 convolution_convert_fusion.8
  160.4 4.3 all-gather.1
  165.0 4.4 sort.17
  169.3 3.7 gather_fusion
  175.8 3.7 gather_fusion.1
  179.5 5.3 scatter_custom_fusion.1
  184.8 5.4 scatter_custom_fusion
  190.6 23.2 %all-gather.17.cloned.1.call-done = bf16[2048,1280]{1,0:T(8,128)(2,1)} async-done(((bf16[128,1280]{1,0:T(8,128)(2,1)}), bf16[2048,1280]{1,0:T(8,128)(2,1)}) %all-gather.17.cloned.1.call-update) | async-done | bytes 5242896 | tf_op jit(solution)/shard_map/all_gather | solution.py:203
  213.8 7.8 copy.136
  221.6 48.9 %all-gather.23.cloned.1.call-done = bf16[2048,1280]{1,0:T(8,128)(2,1)} async-done(((bf16[128,1280]{1,0:T(8,128)(2,1)}), bf16[2048,1280]{1,0:T(8,128)(2,1)}) %all-gather.23.cloned.1.call-update) | async-done | bytes 5242896 | tf_op jit(solution)/shard_map/all_gather | solution.py:204
  270.6 7.9 copy.138
  278.6 25.7 %while.46 = (s32[]{:T(128)}, f32[128,10]{0,1:T(8,128)S(1)}, f32[128,10]{0,1:T(8,128)S(1)}, f32[128,10,128]{2,0,1:T(8,128)S(1)}, s32[16]{0:T(128)S(1)}, /*index=5...) while((s32[]{:T(128)}, f32[128,10]{0,1:T(8,128)S(1)}, ...), condition=%wide.region_6.7_spmd.clone, body=%wide.region_1.6_spmd.clone.sunk | while | flops 85550080 | bytes 5678383 | solution.py:74
  304.6 12.4 all-gather.25.cloned.1.call-done
  320.4 3.8 gather_fusion.2
  325.8 25.8 %all-to-all-start = ((bf16[16,56,1280]{2,1,0:T(8,128)(2,1)}), bf16[16,56,1280]{2,1,0:T(8,128)(2,1)}, u32[]{:S(2)}, u32[]{:S(2)}) async-start(bf16[16,56,1280]{2,1,0:T(8,128)(2,1)} %broadcast_select_fusion), calls=%async_computation | async-start | bytes 4587520 | tf_op jit(solution)/shard_map/all_to_all | solution.py:244
  352.7 4.4 gather_fusion.4
  357.1 4.9 all_gather.63
  363.5 3.7 gather_fusion.5
  367.2 4.0 multiply_convert_fusion.3
  371.2 25.0 %all-to-all-done = bf16[16,56,1280]{2,1,0:T(8,128)(2,1)} async-done(((bf16[16,56,1280]{2,1,0:T(8,128)(2,1)}), bf16[16,56,1280]{2,1,0:T(8,128)(2,1)}, u32[]{:S(2)}, u32[]{:S(2)}) %all-to-all-start) | async-done | bytes 2293792 | tf_op jit(solution)/shard_map/all_to_all | solution.py:244
  396.2 12.0 all-to-all-start.2
  408.9 10.1 fusion.53
  418.9 33.8 %all-to-all-done.2 = bf16[16,56,1280]{2,1,0:T(8,128)(2,1)S(1)} async-done(((bf16[16,56,1280]{2,1,0:T(8,128)(2,1)}), bf16[16,56,1280]{2,1,0:T(8,128)(2,1)S(1)}, u32[]{:S(2)}, u32[]{:S(2)}) %all-to-all-start.2) | async-done | bytes 2293792 | tf_op jit(solution)/shard_map/all_to_all | solution.py:280
  452.8 8.4 fusion.73
  462.3 4.0 convolution_convert_fusion.5
  466.3 12.0 all-to-all-start.1
  480.2 9.0 fusion.56
  489.3 33.5 %all-to-all-done.1 = bf16[16,56,1280]{2,1,0:T(8,128)(2,1)S(1)} async-done(((bf16[16,56,1280]{2,1,0:T(8,128)(2,1)}), bf16[16,56,1280]{2,1,0:T(8,128)(2,1)S(1)}, u32[]{:S(2)}, u32[]{:S(2)}) %all-to-all-start.1) | async-done | bytes 2293792 | tf_op jit(solution)/shard_map/all_to_all | solution.py:255
  522.8 14.0 all-to-all-start.3
  537.4 4.0 fusion.153
  541.4 3.6 multiply_convert_fusion.7
  545.0 4.3 gather_fusion.3
  549.4 4.2 reshape.598
  553.6 48.7 %all-to-all-done.3 = bf16[16,56,1280]{2,1,0:T(8,128)(2,1)} async-done(((bf16[16,56,1280]{2,1,0:T(8,128)(2,1)}), bf16[16,56,1280]{2,1,0:T(8,128)(2,1)}, u32[]{:S(2)}, u32[]{:S(2)}) %all-to-all-start.3) | async-done | bytes 2293792 | tf_op jit(solution)/shard_map/all_to_all | solution.py:304
  602.3 7.9 gather_fusion.6
  613.2 3.3 fusion.97
  619.2 4.0 convolution_add_fusion.5
  630.7 6.1 fusion.64
  636.9 3.5 convolution_convert_fusion.4
  641.8 9.3 fusion.48
  656.3 8.0 copy.154
  664.2 32.4 %all_gather.68 = f32[2048,10]{0,1:T(8,128)} all-gather(f32[128,10]{0,1:T(8,128)S(1)} %log_add_fusion), channel_id=1, replica_groups=mesh['ctx'=16,'fsdp'=2] {'ctx'}, dimensions={0}, use_global_device_ids=true | all-gather | bytes 87040 | tf_op jit(solution)/shard_map/all_gather | solution.py:343
  697.7 35.9 %while.47 = (s32[]{:T(128)}, f32[128,10,128]{2,0,1:T(8,128)S(1)}, s32[16]{0:T(128)}, s32[]{:T(128)}, bf16[16,128,1280]{1,2,0:T(8,128)(2,1)}, /*index=5*/bf16[128...) while((s32[]{:T(128)}, f32[128,10,128]{2,0,1:T(8,128)S(1)}, ...), condition=%wide.region_24.25_spmd.clone, body=%wide.region_20.24_spmd.clone.sunk | while | flops 127653120 | bytes 5980431 | solution.py:74
  734.7 51.5 %all_gather.69 = f32[2048,10]{0,1:T(8,128)} all-gather(f32[128,10]{0,1:T(8,128)S(1)} %get-tuple-element.1448), channel_id=1, replica_groups=mesh['ctx'=16,'fsdp'=2] {'ctx'}, dimensions={0}, use_global_device_ids=true | all-gather | bytes 87040 | tf_op jit(solution)/shard_map/all_gather | solution.py:344
  786.2 7.9 copy.156
  794.2 72.7 %while.48 = (s32[]{:T(128)}, f32[128,10,128]{2,0,1:T(8,128)S(1)}, f32[128,10,128]{0,2,1:T(8,128)S(1)}, s32[16]{0:T(128)S(1)}, s32[]{:T(128)}, /*index=5*/bf16[16...) while((s32[]{:T(128)}, f32[128,10,128]{2,0,1:T(8,128)S(1)}, ...), condition=%wide.region_29.30_spmd.clone, body=%wide.region_25.29_spmd.clone.sunk | while | flops 170743040 | bytes 7956857 | solution.py:74
  804.5 3.3 conditional.11
  849.9 3.4 conditional.11
  879.7 4.1 fusion.155
  889.0 14.0 reduce-scatter.24.cloned.1.call-done
  903.0 4.1 convert_element_type.329
  907.1 43.5 %reduce-scatter.18.cloned.1.call-done = bf16[640,1280]{1,0:T(8,128)(2,1)} async-done(((bf16[1280,1280]{1,0:T(8,128)(2,1)}), bf16[640,1280]{1,0:T(8,128)(2,1)}) %reduce-scatter.18.cloned.1.call-update) | async-done | bytes 1638416 | tf_op jit(solution)/shard_map/reduce_scatter | solution.py:447
  957.2 5.0 all-reduce.3
  963.5 34.8 %reduce-scatter.12.cloned.1.call-done = bf16[640,1280]{1,0:T(8,128)(2,1)} async-done(((bf16[1280,1280]{1,0:T(8,128)(2,1)}), bf16[640,1280]{1,0:T(8,128)(2,1)}) %reduce-scatter.12.cloned.1.call-update) | async-done | bytes 1638416 | tf_op jit(solution)/shard_map/reduce_scatter | solution.py:438
  998.3 47.6 %reduce-scatter.14.cloned.1.call-done = bf16[640,1280]{1,0:T(8,128)(2,1)} async-done(((bf16[1280,1280]{1,0:T(8,128)(2,1)}), bf16[640,1280]{1,0:T(8,128)(2,1)}) %reduce-scatter.14.cloned.1.call-update) | async-done | bytes 1638416 | tf_op jit(solution)/shard_map/reduce_scatter | solution.py:441
  1045.9 47.6 %reduce-scatter.16.cloned.1.call-done = bf16[640,1280]{1,0:T(8,128)(2,1)} async-done(((bf16[1280,1280]{1,0:T(8,128)(2,1)}), bf16[640,1280]{1,0:T(8,128)(2,1)}) %reduce-scatter.16.cloned.1.call-update) | async-done | bytes 1638416 | tf_op jit(solution)/shard_map/reduce_scatter | solution.py:444
  1093.5 417.6 %all-reduce.5 = (f32[640]{0:T(1024)}, f32[640,1280]{1,0:T(8,128)}, f32[640,1280]{1,0:T(8,128)}, f32[640,1280]{1,0:T(8,128)}, f32[640,1280]{1,0:T(8,128)}, /*inde...) all-reduce(f32[640]{0:T(1024)S(1)} %dynamic-slice_convert_fusion.1,, ...), channel_id=1, replica_groups=mesh['ctx'=16,'fsdp'=2] {'ctx'}, use_global_device_ids=true, to_apply=%region_33.34 | all-reduce | flops 5008640 | bytes 30054400 | tf_op jit(solution)/shard_map/psum | solution.py:463
  (550 shorter events, 225.3 us)
Async XLA Ops:
  7.2 7.9 copy-start.2
  7.2 51.5 %all-gather.19.cloned.1.call-start = ((), (), s32[]{:S(2)}) async-start(), calls=%async_computation.15 | async-start | bytes 4915200 | tf_op jit(solution)/shard_map/all_gather | solution.py:116
  7.9 98.8 %all-gather.15.cloned.1.call-start = ((), (), s32[]{:S(2)}) async-start(), calls=%async_computation.13 | async-start | bytes 4915200 | tf_op jit(solution)/shard_map/all_gather | solution.py:117
  8.7 146.0 %all-gather.21.cloned.1.call-start = ((), (), s32[]{:S(2)}) async-start(), calls=%async_computation.16 | async-start | bytes 4915200 | tf_op jit(solution)/shard_map/all_gather | solution.py:118
  9.4 204.4 %all-gather.17.cloned.1.call-start = ((), (), s32[]{:S(2)}) async-start(), calls=%async_computation.14 | async-start | bytes 5570560 | tf_op jit(solution)/shard_map/all_gather | solution.py:203
  14.8 139.9 %copy-start.32 = (f32[1280]{0:T(1024)}, f32[1280]{0:T(1024)S(1)}, u32[]{:S(2)}) copy-start(f32[1280]{0:T(1024)S(1)} %reshape.692) | copy-start | bytes 15364
  15.1 101.9 %copy-start.36 = (f32[128,128]{0,1:T(8,128)}, f32[128,128]{0,1:T(8,128)S(1)}, u32[]{:S(2)}) copy-start(f32[128,128]{0,1:T(8,128)S(1)} %get-tuple-element.1003) | copy-start | bytes 196612
  15.1 101.9 %copy-start.38 = (f32[128,128]{0,1:T(8,128)}, f32[128,128]{0,1:T(8,128)S(1)}, u32[]{:S(2)}) copy-start(f32[128,128]{0,1:T(8,128)S(1)} %get-tuple-element.1004) | copy-start | bytes 196612
  15.8 138.9 %copy-start.41 = (f32[128]{0:T(128)}, f32[128]{0:T(128)S(1)}, u32[]{:S(2)}) copy-start(f32[128]{0:T(128)S(1)} %get-tuple-element.996) | copy-start | bytes 1540
  112.4 3.4 copy-start.10
  117.2 41.4 %copy-start.23 = (bf16[128,10,128]{0,2,1:T(8,128)(2,1)}, bf16[128,10,128]{0,2,1:T(8,128)(2,1)S(1)}, u32[]{:S(2)}) copy-start(bf16[128,10,128]{0,2,1:T(8,128)(2,1)S(1)} %get-tuple-element.986) | copy-start | bytes 983044
  117.3 73.2 %copy-start.25 = (bf16[128,10,128]{0,2,1:T(8,128)(2,1)}, bf16[128,10,128]{0,2,1:T(8,128)(2,1)S(1)}, u32[]{:S(2)}) copy-start(bf16[128,10,128]{0,2,1:T(8,128)(2,1)S(1)} %get-tuple-element.985) | copy-start | bytes 983044
  118.2 152.3 %all-gather.23.cloned.1.call-start = ((), (), s32[]{:S(2)}) async-start(), calls=%async_computation.17 | async-start | bytes 5570560 | tf_op jit(solution)/shard_map/all_gather | solution.py:204
  158.0 2.3 copy-start.47
  158.1 158.9 %all-gather.25.cloned.1.call-start = ((), (), s32[]{:S(2)}) async-start(), calls=%async_computation.18 | async-start | bytes 4915200 | tf_op jit(solution)/shard_map/all_gather | solution.py:119
  158.6 250.2 %all-gather.31.cloned.1.call-start = ((), (), s32[]{:S(2)}) async-start(), calls=%async_computation.21 | async-start | bytes 6881280 | tf_op jit(solution)/shard_map/all_gather | solution.py:239
  159.4 259.5 %all-gather.33.cloned.1.call-start = ((), (), s32[]{:S(2)}) async-start(), calls=%async_computation.22 | async-start | bytes 3440640 | tf_op jit(solution)/shard_map/all_gather | solution.py:240
  160.3 201.9 %copy-start.39 = (s32[1,128,7]{2,1,0:T(8,128)}, s32[1,128,7]{2,1,0:T(8,128)S(1)}, u32[]{:S(2)}) copy-start(s32[1,128,7]{2,1,0:T(8,128)S(1)} %copy.140) | copy-start | bytes 10756
  304.3 15.4 %copy-start = (bf16[128,10,128]{2,0,1:T(8,128)(2,1)}, bf16[128,10,128]{2,0,1:T(8,128)(2,1)S(1)}, u32[]{:S(2)}) copy-start(bf16[128,10,128]{2,0,1:T(8,128)(2,1)S(1)} %get-tuple-element.1375) | copy-start | bytes 983044
  304.5 15.8 %copy-start.15 = (f32[128,10,128]{0,2,1:T(8,128)}, f32[128,10,128]{0,2,1:T(8,128)S(1)}, u32[]{:S(2)}) copy-start(f32[128,10,128]{0,2,1:T(8,128)S(1)} %copy.139) | copy-start | bytes 1966084
  304.6 15.8 %copy-start.17 = (bf16[128,10,128]{0,2,1:T(8,128)(2,1)}, bf16[128,10,128]{0,2,1:T(8,128)(2,1)S(1)}, u32[]{:S(2)}) copy-start(bf16[128,10,128]{0,2,1:T(8,128)(2,1)S(1)} %fusion.115) | copy-start | bytes 983044
  319.6 303.9 %copy-start.5 = (f32[128,1280]{1,0:T(8,128)}, f32[128,1280]{1,0:T(8,128)S(1)}, u32[]{:S(2)}) copy-start(f32[128,1280]{1,0:T(8,128)S(1)} %get-tuple-element.1000) | copy-start | bytes 1966084
  325.8 26.8 %copy-start.21 = (bf16[1,128,1280]{2,1,0:T(8,128)(2,1)S(1)}, bf16[1,128,1280]{2,1,0:T(8,128)(2,1)}, u32[]{:S(2)}) copy-start(bf16[1,128,1280]{2,1,0:T(8,128)(2,1)} %param.41) | copy-start | bytes 983044
  325.8 70.4 %all-to-all-start = ((bf16[16,56,1280]{2,1,0:T(8,128)(2,1)}), bf16[16,56,1280]{2,1,0:T(8,128)(2,1)}, u32[]{:S(2)}, u32[]{:S(2)}) async-start(bf16[16,56,1280]{2,1,0:T(8,128)(2,1)} %broadcast_select_fusion), calls=%async_computation | async-start | bytes 4587520 | tf_op jit(solution)/shard_map/all_to_all | solution.py:244
  351.6 185.7 %all-gather.27.cloned.1.call-start = ((), (), s32[]{:S(2)}) async-start(), calls=%async_computation.19 | async-start | bytes 6881280 | tf_op jit(solution)/shard_map/all_gather | solution.py:122
  352.7 4.4 copy-start.43
  363.2 8.0 copy-start.34
  396.2 56.5 %all-to-all-start.2 = ((bf16[16,56,1280]{2,1,0:T(8,128)(2,1)}), bf16[16,56,1280]{2,1,0:T(8,128)(2,1)S(1)}, u32[]{:S(2)}, u32[]{:S(2)}) async-start(bf16[16,56,1280]{2,1,0:T(8,128)(2,1)} %multiply_convert_fusion.3), calls=%async_computation.2 | async-start | bytes 4587520 | tf_op jit(solution)/shard_map/all_to_all | solution.py:280
  408.2 133.1 %all-gather.29.cloned.1.call-start = ((), (), s32[]{:S(2)}) async-start(), calls=%async_computation.20 | async-start | bytes 3440640 | tf_op jit(solution)/shard_map/all_gather | solution.py:123
  452.8 8.4 copy-start.26
  452.8 9.5 copy-start.50
  466.3 56.5 %all-to-all-start.1 = ((bf16[16,56,1280]{2,1,0:T(8,128)(2,1)}), bf16[16,56,1280]{2,1,0:T(8,128)(2,1)S(1)}, u32[]{:S(2)}, u32[]{:S(2)}) async-start(bf16[16,56,1280]{2,1,0:T(8,128)(2,1)} %convolution_convert_fusion.5), calls=%async_computation.1 | async-start | bytes 4587520 | tf_op jit(solution)/shard_map/all_to_all | solution.py:255
  478.3 178.0 %all-gather.35.cloned.1.call-start = ((), (), s32[]{:S(2)}) async-start(), calls=%async_computation.23 | async-start | bytes 5570560 | tf_op jit(solution)/shard_map/all_gather | solution.py:417
  522.8 79.5 %all-to-all-start.3 = ((bf16[16,56,1280]{2,1,0:T(8,128)(2,1)}), bf16[16,56,1280]{2,1,0:T(8,128)(2,1)}, u32[]{:S(2)}, u32[]{:S(2)}) async-start(bf16[16,56,1280]{2,1,0:T(8,128)(2,1)} %fusion.56), calls=%async_computation.3 | async-start | bytes 4587520 | tf_op jit(solution)/shard_map/all_to_all | solution.py:304
  536.9 249.3 %all-gather.37.cloned.1.call-start = ((), (), s32[]{:S(2)}) async-start(), calls=%async_computation.24 | async-start | bytes 5570560 | tf_op jit(solution)/shard_map/all_gather | solution.py:418
  613.2 3.7 copy-start.40
  613.2 4.3 copy-start.4
  619.1 4.4 copy-start.22
  619.2 4.4 copy-start.49
  623.6 3.5 copy-start.29
  625.1 26.2 %copy-start.12 = (f32[128,1280]{1,0:T(8,128)}, f32[128,1280]{1,0:T(8,128)S(1)}, u32[]{:S(2)}) copy-start(f32[128,1280]{1,0:T(8,128)S(1)} %subtract_add_fusion) | copy-start | bytes 1966084
  627.0 252.7 %reduce-scatter.22.cloned.1.call-start = ((), (), s32[]{:S(2)}) async-start(), calls=%async_computation.30 | async-start | bytes 3440640 | tf_op jit(solution)/shard_map/reduce_scatter | solution.py:459
  629.3 255.8 %reduce-scatter.28.cloned.1.call-start = ((), (), s32[]{:S(2)}) async-start(), calls=%async_computation.33 | async-start | bytes 491520
  630.5 255.7 %reduce-scatter.26.cloned.1.call-start = ((), (), s32[]{:S(2)}) async-start(), calls=%async_computation.32 | async-start | bytes 3440640 | tf_op jit(solution)/shard_map/reduce_scatter | solution.py:309
  636.8 252.1 %reduce-scatter.20.cloned.1.call-start = ((), (), s32[]{:S(2)}) async-start(), calls=%async_computation.29 | async-start | bytes 6881280 | tf_op jit(solution)/shard_map/reduce_scatter | solution.py:456
  640.5 262.6 %reduce-scatter.24.cloned.1.call-start = ((), (), s32[]{:S(2)}) async-start(), calls=%async_computation.31 | async-start | bytes 6881280 | tf_op jit(solution)/shard_map/reduce_scatter | solution.py:306
  651.1 3.7 copy-start.24
  651.1 4.0 copy-start.19
  651.2 299.4 %reduce-scatter.18.cloned.1.call-start = ((), (), s32[]{:S(2)}) async-start(), calls=%async_computation.28 | async-start | bytes 4915200 | tf_op jit(solution)/shard_map/reduce_scatter | solution.py:447
  654.8 343.5 %reduce-scatter.12.cloned.1.call-start = ((), (), s32[]{:S(2)}) async-start(), calls=%async_computation.25 | async-start | bytes 4915200 | tf_op jit(solution)/shard_map/reduce_scatter | solution.py:438
  656.2 40.3 %copy-start.20 = (bf16[128,1280]{1,0:T(8,128)(2,1)S(1)}, bf16[128,1280]{1,0:T(8,128)(2,1)}, u32[]{:S(2)}) copy-start(bf16[128,1280]{1,0:T(8,128)(2,1)} %convolution_convert_fusion.7) | copy-start | bytes 983044
  656.3 40.8 %copy-start.16 = (f32[128,10,128]{0,2,1:T(8,128)S(1)}, f32[128,10,128]{0,2,1:T(8,128)}, u32[]{:S(2)}) copy-start(f32[128,10,128]{0,2,1:T(8,128)} %copy-done.15) | copy-start | bytes 1966084
  664.2 33.5 %copy-start.1 = (bf16[128,10,128]{2,0,1:T(8,128)(2,1)S(1)}, bf16[128,10,128]{2,0,1:T(8,128)(2,1)}, u32[]{:S(2)}) copy-start(bf16[128,10,128]{2,0,1:T(8,128)(2,1)} %copy-done) | copy-start | bytes 983044
  786.2 8.0 copy-start.11
  872.3 173.6 %reduce-scatter.14.cloned.1.call-start = ((), (), s32[]{:S(2)}) async-start(), calls=%async_computation.26 | async-start | bytes 4915200 | tf_op jit(solution)/shard_map/reduce_scatter | solution.py:441
  875.2 218.3 %reduce-scatter.16.cloned.1.call-start = ((), (), s32[]{:S(2)}) async-start(), calls=%async_computation.27 | async-start | bytes 4915200 | tf_op jit(solution)/shard_map/reduce_scatter | solution.py:444
  875.5 2.9 copy-start.51
  875.6 4.2 copy-start.35
  878.4 5.5 copy-start.6
  879.7 4.2 copy-start.27
  950.6 3.3 copy-start.7
  955.8 6.6 copy-start.13
  955.8 6.6 copy-start.48
  955.8 137.7 %copy-start.28 = (bf16[448,1280]{1,0:T(8,128)(2,1)S(1)}, bf16[448,1280]{1,0:T(8,128)(2,1)}, u32[]{:S(2)}) copy-start(bf16[448,1280]{1,0:T(8,128)(2,1)} %reduce-scatter.22.cloned.1.call-done) | copy-start | bytes 3440644
  (15 other events, 23.5 us)
Sparse Core Ops, SparseCore 0:
  9.6 49.0 all-gather.18
  60.3 46.4 all-gather.14
  108.3 46.3 all-gather.20
  157.4 56.3 all-gather.16
  216.0 54.5 all-gather.22
  272.0 44.9 all-gather.24
  318.5 61.6 all-gather.30
  381.7 35.3 all-gather.32
  418.6 61.1 all-gather.26
  481.2 35.3 all-gather.28
  519.5 87.8 all-gather.34
  627.2 66.1 all-gather.36
  696.2 32.6 reduce-scatter.21
  731.1 12.3 reduce-scatter.27
  746.2 34.0 reduce-scatter.25
  783.1 58.5 reduce-scatter.19
  844.4 58.5 reduce-scatter.23
  905.8 44.7 reduce-scatter.17
  953.4 44.8 reduce-scatter.11
  1001.1 44.7 reduce-scatter.13
  1048.7 44.7 reduce-scatter.15
where the time goes:
time: 1530 us; the launch traced here: 1520 us
  waiting for transfers between devices  540 us (35%)
  blocking collectives  521 us (34%)
  local copies, waits for them, and re-layouts  171 us (11%)
  matrix products  127 us (8%)
  starting transfers between devices  65.8 us (4%)
  other arithmetic  42.2 us (3%)
  loops' own time  34.6 us (2%)
  between operations  16.5 us (1%)
    psum x1, blocking collectives, on_device(): lax.psum((summed[0], summed[1], summed[2], summed[3], summed[4], summed[5...  418 us
    dynamic_slice x68, local copies, waits for them, and re-layouts, over_shards(): lax.scan(visit, carry, (parts, jnp.arange(count, dtype=jnp.int32)))  61.6 us
    all_gather x1, blocking collectives, on_device(): lax.all_gather(delta, 'ctx', axis=0, tiled=True)  51.5 us
    all_gather x1, waiting for transfers between devices, on_device(): lax.all_gather(value_rows.reshape(tokens, width), 'ctx', axis=0, tiled=True)  48.9 us
    all_to_all x1, waiting for transfers between devices, on_device(): lax.all_to_all(grad_rows_in, 'ctx', split_axis=0, concat_axis=0, tiled=True)  48.7 us
    reduce_scatter x1, waiting for transfers between devices, on_device(): lax.psum_scatter(grad_value_w.astype(jnp.bfloat16), 'fsdp', scatter_dimen...  47.6 us
    reduce_scatter x1, waiting for transfers between devices, on_device(): lax.psum_scatter(grad_key_w.astype(jnp.bfloat16), 'fsdp', scatter_dimensi...  47.6 us
    reduce_scatter x1, waiting for transfers between devices, on_device(): lax.psum_scatter(grad_output_w.astype(jnp.bfloat16), 'fsdp', scatter_dime...  43.5 us
  transfers between devices with their start and end apart: 25, of which 15 were waited for; matrix products, arithmetic and copies ran while one was open for 22% of the time, Pallas kernels for 0%

commit v1 on v0

v1 whole, which is shorter than its diff:
```python
import functools
import math

import jax
import jax.numpy as jnp
from jax import lax
from jax.experimental import pallas as pl
from jax.experimental.pallas import tpu as pltpu
from jax.sharding import PartitionSpec as P

HEADS = 10
HEAD_DIM = 128
EXP_HID = 896
TOP = 7
BLOCK = 256
TILE = 512

epsilon = 1e-06
masked_score = -1000000000.0
score_scale = 1.0 / math.sqrt(HEAD_DIM)
exact = lax.Precision.HIGHEST
f32 = jnp.float32
bf16 = jnp.bfloat16


def dot(a, b):
    return jnp.dot(a, b, preferred_element_type=f32)


def dot_nt(a, b):
    return lax.dot_general(a, b, (((1,), (1,)), ((), ())), preferred_element_type=f32)


def dot_tn(a, b):
    return lax.dot_general(a, b, (((0,), (0,)), ((), ())), preferred_element_type=f32)


def rms_scale(values):
    return lax.rsqrt(jnp.mean(values * values, axis=-1, keepdims=True) + epsilon)


def rotary_tables(positions, width):
    half = width // 2
    freqs = jnp.exp(-math.log(10000.0) * jnp.arange(half, dtype=f32) * 2.0 / width)
    angles = positions.astype(f32)[:, None] * freqs[None, :]
    cosine = jnp.concatenate([jnp.cos(angles), jnp.cos(angles)], axis=-1)
    sine = jnp.concatenate([jnp.sin(angles), jnp.sin(angles)], axis=-1)
    return (cosine, sine)


def rotate(values, cosine, sine):
    half = values.shape[-1] // 2
    turned = jnp.concatenate([-values[..., half:], values[..., :half]], axis=-1)
    return values * cosine + turned * sine


def rotate_back(grads, cosine, sine):
    half = grads.shape[-1] // 2
    scaled = grads * sine
    return grads * cosine + jnp.concatenate([scaled[..., half:], -scaled[..., :half]], axis=-1)


def allowed_tile(rows, columns):
    key_block = lax.broadcasted_iota(jnp.int32, (rows, columns), 0) // BLOCK
    query_block = lax.broadcasted_iota(jnp.int32, (rows, columns), 1) // BLOCK
    return key_block <= query_block


def attend_kernel(q_ref, k_ref, v_ref, context_ref, lse_ref, score_ref):
    tile = q_ref.shape[0]
    here = pl.program_id(0)
    queries = q_ref[...]

    def raw_scores(j):
        keys = k_ref[pl.ds(pl.multiple_of(j * tile, tile), tile), :]
        return dot_nt(keys, queries) * score_scale

    def fold(j, scores, peak):
        score_ref[pl.ds(pl.multiple_of(j * tile, tile), tile), :] = scores
        return jnp.maximum(peak, jnp.max(scores.reshape(tile // 8, 8, tile), axis=0))

    diagonal = jnp.where(allowed_tile(tile, tile), raw_scores(here), masked_score)
    peak = fold(here, diagonal, jnp.full((8, tile), masked_score, f32))
    peak = lax.fori_loop(0, here, lambda j, p: fold(j, raw_scores(j), p), peak)
    top = jnp.max(peak, axis=0, keepdims=True)

    def gather(j, carry):
        total, numer = carry
        window = pl.ds(pl.multiple_of(j * tile, tile), tile)
        weights = jnp.exp(score_ref[window, :] - top)
        total = total + jnp.sum(weights.reshape(tile // 8, 8, tile), axis=0)
        return total, numer + dot_tn(v_ref[window, :], weights.astype(bf16))

    zero = (jnp.zeros((8, tile), f32), jnp.zeros((HEAD_DIM, tile), f32))
    total, numer = lax.fori_loop(0, here + 1, gather, zero)
    total = jnp.sum(total, axis=0, keepdims=True)
    context_ref[...] = (numer / total).T
    lse_ref[...] = top + jnp.log(total)


def attend(query, key, value):
    length = query.shape[0]
    tile = min(TILE, length)
    whole = pl.BlockSpec((length, HEAD_DIM), lambda i: (0, 0))
    part = pl.BlockSpec((tile, HEAD_DIM), lambda i: (i, 0))
    return pl.pallas_call(
        attend_kernel,
        grid=(length // tile,),
        in_specs=[part, whole, whole],
        out_specs=[part, pl.BlockSpec((1, tile), lambda i: (0, i))],
        out_shape=[
            jax.ShapeDtypeStruct((length, HEAD_DIM), f32),
            jax.ShapeDtypeStruct((1, length), f32),
        ],
        scratch_shapes=[pltpu.VMEM((length, tile), f32)],
        name="attend",
        cost_estimate=pl.CostEstimate(
            flops=2 * length * length * HEAD_DIM,
            bytes_accessed=12 * length * HEAD_DIM,
            transcendentals=length * length // 2,
        ),
    )(query, key, value)


def attend_back_kernel(
    q_ref, grad_ref, lse_ref, delta_ref, k_ref, v_ref, dq_ref, dk_ref, dv_ref
):
    tile = k_ref.shape[0]
    here = pl.program_id(0)
    keys = k_ref[...]
    values = v_ref[...]

    @pl.when(here == 0)
    def _():
        dq_ref[...] = jnp.zeros_like(dq_ref)

    def visit(i, masked):
        window = pl.ds(pl.multiple_of(i * tile, tile), tile)
        queries = q_ref[window, :]
        grads = grad_ref[window, :]
        weights = jnp.exp(dot_nt(keys, queries) * score_scale - lse_ref[:, window])
        if masked:
            weights = jnp.where(allowed_tile(tile, tile), weights, 0.0)
        grad_weights = dot_nt(values, grads)
        grad_raw = (weights * (grad_weights - delta_ref[:, window]) * score_scale).astype(bf16)
        dq_ref[window, :] += dot_tn(grad_raw, keys)
        return dot(grad_raw, queries), dot(weights.astype(bf16), grads)

    dk, dv = visit(here, True)
    dk_ref[...] = dk
    dv_ref[...] = dv

    def step(i, carry):
        more_k, more_v = visit(i, False)
        dk_ref[...] += more_k
        dv_ref[...] += more_v
        return carry

    lax.fori_loop(here + 1, pl.num_programs(0), step, 0)


def attend_back(query, key, value, grad, lse, delta):
    length = query.shape[0]
    tile = min(TILE, length)
    whole = pl.BlockSpec((length, HEAD_DIM), lambda i: (0, 0))
    row = pl.BlockSpec((1, length), lambda i: (0, 0))
    part = pl.BlockSpec((tile, HEAD_DIM), lambda i: (i, 0))
    return pl.pallas_call(
        attend_back_kernel,
        grid=(length // tile,),
        in_specs=[whole, whole, row, row, part, part],
        out_specs=[whole, part, part],
        out_shape=[jax.ShapeDtypeStruct((length, HEAD_DIM), f32)] * 3,
        name="attend_back",
        cost_estimate=pl.CostEstimate(
            flops=5 * length * length * HEAD_DIM,
            bytes_accessed=20 * length * HEAD_DIM,
            transcendentals=length * length // 2,
        ),
    )(query, grad, lse, delta, key, value)


def swiglu_back(grad_hidden, gate_part, up_part):
    sigmoid = jax.nn.sigmoid(gate_part)
    grad_gate = grad_hidden * up_part * sigmoid * (1.0 + gate_part * (1.0 - sigmoid))
    grad_up = grad_hidden * jax.nn.silu(gate_part)
    return jnp.concatenate([grad_gate, grad_up], axis=-1).astype(bf16)


def slot_table(span_picks, span_order, experts):
    tokens = span_picks.shape[0]
    order = span_order.reshape(tokens, TOP)
    onehot = span_picks[:, :, None] == jnp.arange(experts, dtype=jnp.int32)
    picked = jnp.any(onehot, axis=1)
    rank_key = jnp.sum(jnp.where(onehot, order[:, :, None], 0), axis=1)
    rank_key = jnp.where(picked, rank_key, tokens * TOP)
    before = rank_key[:, None, :] < rank_key[None, :, :]
    slots = jnp.sum(before.astype(jnp.int32), axis=0)
    return jnp.where(picked, slots, tokens * TOP)


def on_device(
    inputs,
    norm1_gain,
    w_query,
    w_key,
    w_value,
    w_output,
    norm2_gain,
    router,
    shared_gate_up_weight,
    shared_down_weight,
    expert_in,
    expert_out,
    picks,
    fill_order,
    grad_out,
):
    spans = lax.axis_size("ctx")
    here = lax.axis_index("ctx")
    side = lax.axis_index("fsdp")
    tokens, width = inputs.shape[1:]
    half = width // 2
    length = spans * tokens
    experts = spans * expert_in.shape[0]
    capacity = tokens * TOP // experts
    head = jnp.minimum(here, HEADS - 1)
    share = shared_down_weight.shape[0] // spans

    def across(value):
        return lax.ppermute(value, "fsdp", [(0, 1), (1, 0)])

    def ordered(own, other, axis):
        return jnp.where(
            side == 0,
            jnp.concatenate([own, other], axis=axis),
            jnp.concatenate([other, own], axis=axis),
        )

    def both(own, axis=0):
        return ordered(own, across(own), axis)

    def everyone(value):
        return lax.all_gather(value, "ctx", axis=0, tiled=True)

    def columns(value, start, count):
        return lax.dynamic_slice_in_dim(value, start, count, 1)

    def rows(value, start, count):
        return lax.dynamic_slice_in_dim(value, start, count, 0)

    def halves(value, axis=0):
        size = value.shape[axis] // 2
        mine = lax.dynamic_slice_in_dim(value, side * size, size, axis)
        theirs = lax.dynamic_slice_in_dim(value, (1 - side) * size, size, axis)
        return mine, theirs

    def reduced(value, axis=0):
        mine, theirs = halves(value, axis)
        return mine + across(theirs.astype(bf16)).astype(f32)

    x_all = everyone(inputs[0])
    g_all = everyone(grad_out[0])

    table = everyone(slot_table(picks[0], fill_order[0, 0], experts))
    head_parts = [columns(w, head * HEAD_DIM, HEAD_DIM) for w in (w_query, w_key, w_value)]
    small = jnp.concatenate(
        head_parts + [router, norm1_gain[:, None], norm2_gain[:, None]], axis=1
    )
    small = both(small)
    head_w = small[:, : 3 * HEAD_DIM]
    router_w = small[:, 3 * HEAD_DIM : 3 * HEAD_DIM + experts]
    gain_one = small[:, 3 * HEAD_DIM + experts].astype(f32)
    gain_two = small[:, 3 * HEAD_DIM + experts + 1].astype(f32)
    output_w = both(w_output)
    starts = [part * EXP_HID + block * (EXP_HID // 2) for part in (0, 1) for block in (0, 1)]
    shared_in = both(
        jnp.concatenate(
            [columns(shared_gate_up_weight, s + here * share, share) for s in starts], axis=1
        )
    )
    shared_out = both(rows(shared_down_weight, here * share, share))
    expert_in_w = both(expert_in[0])
    expert_out_w = both(expert_out[0])
    query_other, key_other, value_other = (across(w) for w in (w_query, w_key, w_value))

    cosine, sine = rotary_tables(jnp.arange(length, dtype=jnp.int32), HEAD_DIM)

    resid_all = x_all.astype(f32)
    normed1_all = (resid_all * rms_scale(resid_all) * gain_one).astype(bf16)
    projected = dot(normed1_all, head_w)
    query = rotate(projected[:, :HEAD_DIM], cosine, sine).astype(bf16)
    key = rotate(projected[:, HEAD_DIM : 2 * HEAD_DIM], cosine, sine).astype(bf16)
    value = projected[:, 2 * HEAD_DIM :].astype(bf16)
    context, lse = attend(query, key, value)
    attended_head = context.astype(bf16)

    def to_tokens(rows_of_head):
        sent = rows_of_head.reshape(spans, tokens, -1)
        got = lax.all_to_all(sent, "ctx", split_axis=0, concat_axis=0, tiled=True)
        return got[:HEADS]

    def by_token(got):
        return jnp.swapaxes(got, 0, 1).reshape(tokens, -1)

    attended = by_token(to_tokens(attended_head))
    resid = inputs[0].astype(f32)
    second = resid + dot(attended, output_w)
    scale_two = rms_scale(second)
    normed2 = (second * scale_two * gain_two).astype(bf16)
    normed2_all = everyone(normed2)

    logits = dot(normed2_all, router_w)
    picked = table < tokens * TOP
    peak = jnp.max(jnp.where(picked, logits, masked_score), axis=-1, keepdims=True)
    chances = jnp.where(picked, jnp.exp(logits - peak), 0.0)
    gates = chances / jnp.sum(chances, axis=-1, keepdims=True)
    expert_ids = lax.broadcasted_iota(jnp.int32, (length, experts), 1)
    own_slot = jnp.sum(jnp.where(expert_ids == here, table, 0), axis=1).reshape(spans, tokens)
    own_gate = jnp.sum(jnp.where(expert_ids == here, gates, 0.0), axis=1).reshape(spans, tokens)
    takes = own_slot[:, None, :] == jnp.arange(capacity, dtype=jnp.int32)[None, :, None]
    select = takes.astype(bf16)
    slot_gate = jnp.sum(jnp.where(takes, own_gate[:, None, :], 0.0), axis=2).reshape(-1, 1)

    def to_slots(value):
        picked_rows = jnp.einsum(
            "rst,rtd->rsd",
            select,
            value.reshape(spans, tokens, width),
            preferred_element_type=bf16,
        )
        return picked_rows.reshape(spans * capacity, width)

    def from_slots(value):
        back = jnp.einsum(
            "rst,rsd->rtd",
            select,
            value.reshape(spans, capacity, width),
            preferred_element_type=f32,
        )
        return back.reshape(length, width)

    dispatched = to_slots(normed2_all)
    grad_slots = to_slots(g_all)
    projected_e = dot(dispatched, expert_in_w)
    gate_e, up_e = projected_e[:, :EXP_HID], projected_e[:, EXP_HID:]
    expert_hidden = (jax.nn.silu(gate_e) * up_e).astype(bf16)
    expert_result = dot(expert_hidden, expert_out_w).astype(bf16)
    grad_slots_f = grad_slots.astype(f32)
    grad_result = (grad_slots_f * slot_gate).astype(bf16)
    slot_dot = jnp.sum(grad_slots_f * expert_result.astype(f32), axis=1).reshape(spans, capacity)
    gate_dot = jnp.sum(jnp.where(takes, slot_dot[:, :, None], 0.0), axis=1)
    gate_grads = lax.all_to_all(
        gate_dot[:, None, :], "ctx", split_axis=0, concat_axis=0, tiled=True
    )[:, 0, :].T

    shared_proj = dot(normed2_all, shared_in)
    shared_gate, shared_up = shared_proj[:, : 2 * share], shared_proj[:, 2 * share :]
    shared_hidden = (jax.nn.silu(shared_gate) * shared_up).astype(bf16)
    out_part = from_slots(expert_result) * own_gate.reshape(-1, 1) + dot(shared_hidden, shared_out)

    grad_ehidden = dot_nt(grad_result, expert_out_w)
    grad_eproj = swiglu_back(grad_ehidden, gate_e, up_e)
    grad_dispatched = dot_nt(grad_eproj, expert_in_w).astype(bf16)
    grad_shidden = dot_nt(g_all, shared_out)
    grad_sproj = swiglu_back(grad_shidden, shared_gate, shared_up)
    grad_part = from_slots(grad_dispatched) + dot_nt(grad_sproj, shared_in)
    scatter = functools.partial(lax.psum_scatter, axis_name="ctx", scatter_dimension=0, tiled=True)
    grad_normed2 = scatter(grad_part.astype(bf16)).astype(f32)

    grad_expert_out = reduced(dot_tn(expert_hidden, grad_result))
    grad_expert_in = reduced(dot_tn(dispatched, grad_eproj))
    grad_shared_in = reduced(dot_tn(normed2_all, grad_sproj)).astype(bf16)
    grad_shared_out = reduced(dot_tn(shared_hidden, g_all)).astype(bf16)

    own_gates = rows(gates, here * tokens, tokens)
    grad_sel = own_gates * (gate_grads - jnp.sum(own_gates * gate_grads, axis=-1, keepdims=True))
    grad_logits = grad_sel.astype(bf16)
    grad_normed2 = grad_normed2 + dot_nt(grad_logits, router_w)
    norm2_part = jnp.sum(grad_normed2 * second * scale_two, axis=0)
    hat = grad_normed2 * gain_two
    cubed = scale_two * scale_two * scale_two
    grad_second = (
        grad_out[0].astype(f32)
        + scale_two * hat
        - second * cubed * jnp.mean(hat * second, axis=-1, keepdims=True)
    )
    grad_mixed = grad_second.astype(bf16)
    grad_context = dot_nt(grad_mixed, output_w).astype(bf16)

    grad_context_head = jnp.swapaxes(grad_context.reshape(tokens, HEADS, HEAD_DIM), 0, 1)
    grad_context_head = jnp.pad(grad_context_head, ((0, spans - HEADS), (0, 0), (0, 0)))
    grad_context_head = lax.all_to_all(
        grad_context_head, "ctx", split_axis=0, concat_axis=0, tiled=True
    ).reshape(length, HEAD_DIM)

    high = norm2_part.astype(bf16)
    low = (norm2_part - high.astype(f32)).astype(bf16)
    extra_rows = jnp.zeros((16, width), bf16).at[0].set(high).at[1].set(low)
    extra_columns = jnp.pad(grad_logits, ((0, 16), (0, HEAD_DIM - experts)))
    carried = jnp.concatenate(
        [jnp.concatenate([grad_mixed, extra_rows], axis=0), extra_columns], axis=1
    )
    carried = everyone(carried).reshape(spans, tokens + 16, width + HEAD_DIM)
    grad_mixed_all = carried[:, :tokens, :width].reshape(length, width)
    grad_logits_all = carried[:, :tokens, width : width + experts].reshape(length, experts)
    norm2_all = jnp.sum(carried[:, tokens : tokens + 2, :width].astype(f32), axis=(0, 1))
    grad_norm2 = reduced_f32 = None
    mine, theirs = halves(norm2_all)
    grad_norm2 = mine + across(theirs)
    grad_router = dot_tn(normed2_all, grad_logits_all)
    mine, theirs = halves(grad_router)
    grad_router = mine + across(theirs)
    grad_output = dot_tn(attended_head, grad_mixed_all).astype(bf16)
    grad_output = (grad_output.astype(f32) + across(grad_output).astype(f32)).astype(bf16)

    delta = jnp.sum(grad_context_head.astype(f32) * context, axis=-1).reshape(1, length)
    grad_q, grad_k, grad_v = attend_back(query, key, value, grad_context_head, lse, delta)
    grad_heads = jnp.concatenate(
        [rotate_back(grad_q, cosine, sine), rotate_back(grad_k, cosine, sine), grad_v], axis=1
    ).astype(bf16)
    grad_head_w = reduced(dot_tn(normed1_all, grad_heads)).astype(bf16)

    got = to_tokens(grad_heads)
    pieces = [
        by_token(got[:, :, i * HEAD_DIM : (i + 1) * HEAD_DIM]) for i in range(3)
    ]
    own_part = sum(dot_nt(p, w) for p, w in zip(pieces, (w_query, w_key, w_value)))
    other_part = sum(dot_nt(p, w) for p, w in zip(pieces, (query_other, key_other, value_other)))
    grad_normed1 = ordered(own_part, other_part, 1)
    scale_one = rms_scale(resid)
    hat = grad_normed1 * gain_one
    cubed = scale_one * scale_one * scale_one
    grad_inputs = (
        grad_second
        + scale_one * hat
        - resid * cubed * jnp.mean(hat * resid, axis=-1, keepdims=True)
    )

    def replicated(value):
        return everyone(value[None])

    grads_qkv = replicated(grad_head_w)[:HEADS].reshape(HEADS, half, 3, HEAD_DIM)
    grad_query, grad_key, grad_value = (
        jnp.swapaxes(grads_qkv[:, :, i], 0, 1).reshape(half, width).astype(f32) for i in range(3)
    )
    gain_products = (
        grad_query * w_query.astype(f32)
        + grad_key * w_key.astype(f32)
        + grad_value * w_value.astype(f32)
    )
    grad_norm1 = jnp.sum(gain_products, axis=1) / norm1_gain.astype(f32)
    side_heads = HEADS // 2
    grad_output = rows(replicated(grad_output), side * side_heads, side_heads)
    grad_output = grad_output.reshape(half, width).astype(f32)
    grad_shared_in = replicated(grad_shared_in).reshape(spans, half, 4, share)
    grad_shared_in = jnp.transpose(grad_shared_in, (1, 2, 0, 3)).reshape(half, 2 * EXP_HID)
    grad_shared_out = everyone(grad_shared_out)
    layer_out = second + scatter(out_part.astype(bf16)).astype(f32)
    return (
        layer_out.astype(bf16)[None],
        grad_inputs[None],
        grad_norm1,
        grad_query,
        grad_key,
        grad_value,
        grad_output,
        grad_norm2,
        grad_router,
        grad_shared_in.astype(f32),
        grad_shared_out.astype(f32),
        grad_expert_in[None],
        grad_expert_out[None],
    )


def solution(mesh):
    placed = (
        P("fsdp", "ctx", None),
        P("fsdp"),
        P("fsdp", None),
        P("fsdp", None),
        P("fsdp", None),
        P("fsdp", None),
        P("fsdp"),
        P("fsdp", None),
        P("fsdp", None),
        P("fsdp", None),
        P("ctx", "fsdp", None),
        P("ctx", "fsdp", None),
        P("fsdp", "ctx", None),
        P("fsdp", "ctx", None),
        P("fsdp", "ctx", None),
    )
    return jax.shard_map(
        on_device,
        mesh=mesh,
        in_specs=placed,
        out_specs=(
            P("fsdp", "ctx", None),
            P("fsdp", "ctx", None),
            P("fsdp"),
            P("fsdp", None),
            P("fsdp", None),
            P("fsdp", None),
            P("fsdp", None),
            P("fsdp"),
            P("fsdp", None),
            P("fsdp", None),
            P("fsdp", None),
            P("ctx", "fsdp", None),
            P("ctx", "fsdp", None),
        ),
        check_vma=False,
    )
```

time: 1530 us -> 815 us (0.53)
  blocking collectives: 521 us -> 57.5 us
  waiting for transfers between devices: 540 us -> 355 us
  local copies, waits for them, and re-layouts: 171 us -> 113 us
  other arithmetic: 42.2 us -> 79 us
  loops' own time: 34.6 us -> 0 us
  starting transfers between devices: 65.8 us -> 38.2 us
  Pallas kernels: 0 us -> 23.1 us
    psum x1 -> x0, blocking collectives: 418 us -> none  [on_device(): lax.psum((summed[0], summed[1], summed[2], summed[3], summed[4], summed[5...]
    all_gather x12 -> x8, waiting for transfers between devices: 206 us -> 49.4 us  [everyone(): return lax.all_gather(value, 'ctx', axis=0, tiled=True)]
    ppermute x0 -> x17, waiting for transfers between devices: none -> 150 us  [across(): return lax.ppermute(value, 'fsdp', [(0, 1), (1, 0)])]
    all_to_all x4 -> x3, waiting for transfers between devices: 141 us -> 18.1 us  [the longest x1 11.8 us: on_device(): lax.all_to_all(grad_context_head, 'ctx', split_axis=0, concat_axis=0, til...]
    all_gather x5 -> x1, blocking collectives: 98.4 us -> 31.1 us  [everyone(): return lax.all_gather(value, 'ctx', axis=0, tiled=True)]
    dynamic_slice x68 -> x8, local copies, waits for them, and re-layouts: 61.6 us -> 5.25 us  [the longest x4 3.51 us: columns(): return lax.dynamic_slice_in_dim(value, start, count, 1)]
    reduce_scatter x8 -> x2, waiting for transfers between devices: 188 us -> 136 us  [the longest x1 78.8 us: on_device(): layer_out = second + scatter(out_part.astype(bf16)).astype(f32)]
    all_to_all x4 -> x3, starting transfers between devices: 63.9 us -> 17.5 us  [the longest x1 9.68 us: to_tokens(): got = lax.all_to_all(sent, 'ctx', split_axis=0, concat_axis=0, tiled=True)]
  transfers between devices with their start and end apart: 25 -> 30, of which waited for: 15 -> 16; matrix products, arithmetic and copies ran while one was open for 22% -> 36% of each run, Pallas kernels for 0% -> 3%
where the time goes in v1:
time: 815 us; the launch traced here: 799 us
  waiting for transfers between devices  355 us (44%)
  matrix products  118 us (14%)
  local copies, waits for them, and re-layouts  113 us (14%)
  other arithmetic  79 us (10%)
  blocking collectives  57.5 us (7%)
  starting transfers between devices  38.2 us (5%)
  Pallas kernels  23.1 us (3%)
  between operations  15.5 us (2%)
    ppermute x17, waiting for transfers between devices, across(): return lax.ppermute(value, 'fsdp', [(0, 1), (1, 0)])  150 us
    reduce_scatter x1, waiting for transfers between devices, on_device(): layer_out = second + scatter(out_part.astype(bf16)).astype(f32)  78.8 us
    reduce_scatter x1, waiting for transfers between devices, on_device(): grad_normed2 = scatter(grad_part.astype(bf16)).astype(f32)  57.4 us
    all_gather x8, waiting for transfers between devices, everyone(): return lax.all_gather(value, 'ctx', axis=0, tiled=True)  49.4 us
    dot_general x12, matrix products, dot_nt(): lax.dot_general(a, b, (((1,), (1,)), ((), ())), preferred_element_type=f32)  44.1 us
    unnamed x125, local copies, waits for them, and re-layouts  39.1 us
    dot_general x7, matrix products, dot(): return jnp.dot(a, b, preferred_element_type=f32)  31.1 us
    all_gather x1, blocking collectives, everyone(): return lax.all_gather(value, 'ctx', axis=0, tiled=True)  31.1 us
  transfers between devices with their start and end apart: 30, of which 16 were waited for; matrix products, arithmetic and copies ran while one was open for 36% of the time, Pallas kernels for 3%

profile of v1, /device:TPU:0, one launch (start us, length us, event | category | flops | bytes accessed | tf_op | source)
XLA Modules:
  0.0 799.3 jit_solution(5684408631827278898)
XLA Ops:
  8.7 2.9 copy.112
  11.6 4.1 copy.113
  15.8 3.5 copy.114
  21.3 3.3 concatenate.98
  24.6 3.0 collective-permute-start
  27.6 3.7 multiply_cosine_fusion
  31.3 9.3 %collective-permute-done = bf16[640,402]{0,1:T(8,128)(2,1)} collective-permute-done((bf16[640,402]{0,1:T(8,128)(2,1)}, bf16[640,402]{0,1:T(8,128)(2,1)}, u32[]{:S(2)}, u32[]{:S(2)}) %collective-permute-start) | collective-permute-done | bytes 514592 | tf_op jit(solution)/shard_map/ppermute | solution.py:231
  43.6 25.4 %all-gather.19.cloned.1.call-done = bf16[1,2048,1280]{2,1,0:T(8,128)(2,1)} async-done(((bf16[1,128,1280]{2,1,0:T(8,128)(2,1)}), bf16[1,2048,1280]{2,1,0:T(8,128)(2,1)}) %all-gather.19.cloned.1.call-update) | async-done | bytes 5242896 | tf_op jit(solution)/shard_map/all_gather | solution.py:244
  69.0 3.7 fusion
  73.1 4.2 fusion.24
  81.0 9.5 %attend.1 = (f32[2048,128]{1,0:T(8,128)}, f32[1,2048]{1,0:T(1,128)}) custom-call(bf16[2048,128]{1,0:T(8,128)(2,1)} %get-tuple-element.106.q_ref, bf16[2048,128]{1,0:T(8,128)(2,1)} %get-tuple-element.105.k_ref, bf16[2048,128]{1,0:T(8,128)(2,1)} %slice.236.v_ref), custom_call_target="tpu_custom_call" | custom-call | flops 1073741824 | bytes 3145728 | tf_op jit(solution)/shard_map/attend/pallas_call | solution.py:106
  94.6 26.4 %all_to_all.20 = bf16[16,128,128]{1,2,0:T(8,128)(2,1)S(1)} all-to-all(bf16[16,128,128]{1,2,0:T(8,128)(2,1)} %copy.122), channel_id=1, replica_groups=mesh['ctx'=16,'fsdp'=2] {'ctx'}, dimensions={0} | all-to-all | bytes 1048576 | tf_op jit(solution)/shard_map/all_to_all | solution.py:300
  121.0 4.5 multiply_reduce_fusion.3
  135.8 31.1 %all_gather.28 = s32[2048,16]{1,0:T(8,128)S(1)} all-gather(s32[128,16]{1,0:T(8,128)S(1)} %broadcast_select_fusion), channel_id=1, replica_groups=mesh['ctx'=16,'fsdp'=2] {'ctx'}, dimensions={0}, use_global_device_ids=true | all-gather | bytes 139264 | tf_op jit(solution)/shard_map/all_gather | solution.py:244
  167.3 5.3 fusion.49
  172.6 23.9 %all-gather.15.cloned.1.call-done = bf16[2048,1280]{1,0:T(8,128)(2,1)} async-done(((bf16[128,1280]{1,0:T(8,128)(2,1)}), bf16[2048,1280]{1,0:T(8,128)(2,1)}) %all-gather.15.cloned.1.call-update) | async-done | bytes 5242896 | tf_op jit(solution)/shard_map/all_gather | solution.py:244
  196.6 3.5 fusion.51
  201.5 6.8 fusion.35
  215.7 5.6 fusion.11
  224.4 9.7 %multiply_convert_fusion.1 = (bf16[896,896]{1,0:T(8,128)(2,1)S(1)}, bf16[896,896]{1,0:T(8,128)(2,1)}) fusion(f32[896,1792]{1,0:T(8,128)} %copy-done.6, bf16[896,1280]{1,0:T(8,128)(2,1)S(1)} %fusion.10, bf16[448,1280]{1,0:T(8,128)(2,1)} %collective-permute-done.3, bf16[448,1280]{1,0:T(8,128)(2,1)} %bitcast.222, pred[]{:T(512)S(6)} %eq.23), kind=kOutput, calls=%fused_computation.31 | convolution fusion | flops 2075967488 | bytes 14221313 | tf_op jit(solution)/shard_map/dot_general | solution.py:31
  234.1 9.3 %convolution_convert_fusion = bf16[896,1280]{1,0:T(8,128)(2,1)} fusion(bf16[896,896]{1,0:T(8,128)(2,1)} %get-tuple-element.101, bf16[896,896]{1,0:T(8,128)(2,1)S(1)} %get-tuple-element.100, bf16[640,1792]{1,0:T(8,128)(2,1)} %collective-permute-done.2, bf16[640,1792]{1,0:T(8,128)(2,1)S(1)} %bitcast.220, pred[]{:T(512)S(6)} %eq.23), kind=kOutput, calls=%fused_computation.22 | convolution fusion | flops 4138631168 | bytes 10092545 | tf_op jit(solution)/shard_map/dot_general | solution.py:31
  243.4 3.5 fusion.48
  247.0 2.9 fusion.82
  249.9 2.7 multiply_convert_fusion.5
  253.3 5.1 fusion.3
  258.4 3.2 fusion.50
  261.7 4.6 fusion.5
  266.3 3.6 all-to-all-start.1
  270.0 6.2 all-to-all-done.1
  278.3 57.4 %reduce-scatter.5.cloned.1.call-done = bf16[128,1280]{1,0:T(8,128)(2,1)} async-done(((bf16[2048,1280]{1,0:T(8,128)(2,1)}), bf16[128,1280]{1,0:T(8,128)(2,1)}) %reduce-scatter.5.cloned.1.call-update) | async-done | bytes 327696 | tf_op jit(solution)/shard_map/reduce_scatter | solution.py:369
  338.0 78.8 %reduce-scatter.3.cloned.1.call-done = bf16[128,1280]{1,0:T(8,128)(2,1)} async-done(((bf16[2048,1280]{1,0:T(8,128)(2,1)}), bf16[128,1280]{1,0:T(8,128)(2,1)}) %reduce-scatter.3.cloned.1.call-update) | async-done | bytes 327696 | tf_op jit(solution)/shard_map/reduce_scatter | solution.py:459
  420.2 3.7 fusion.8
  425.4 3.1 collective-permute-done.14
  429.2 4.3 fusion.55
  433.5 3.9 convolution_convert_fusion.2
  441.2 4.2 all-to-all-start.2
  447.9 4.6 collective-permute-done.13
  454.2 11.8 %all-to-all-done.2 = bf16[16,128,128]{1,2,0:T(8,128)(2,1)} async-done(((bf16[16,128,128]{1,2,0:T(8,128)(2,1)}), bf16[16,128,128]{1,2,0:T(8,128)(2,1)}, u32[]{:S(2)}, u32[]{:S(2)}) %all-to-all-start.2) | async-done | bytes 524320 | tf_op jit(solution)/shard_map/all_to_all | solution.py:393
  470.1 13.6 %attend_back.1 = (f32[2048,128]{1,0:T(8,128)}, f32[2048,128]{1,0:T(8,128)}, f32[2048,128]{1,0:T(8,128)}) custom-call(bf16[2048,128]{1,0:T(8,128)(2,1)} %get-tuple-element.106.q_ref, bf16[2048,128]{1,0:T(8,128)(2,1)} %bitcast.204, f32[1,2048]{1,0:T(1,128)} %get-tuple-element.43.lse_ref, f32[1,2048]{1,0:T(1,128)} %bitcast.217, ...), custom_call_target="tpu_custom_call" | custom-call | flops 2684354560 | bytes 5242880 | tf_op jit(solution)/shard_map/attend_back/pallas_call | solution.py:168
  490.4 3.1 fusion.17
  494.9 12.0 %collective-permute-done.9 = bf16[640,384]{1,0:T(8,128)(2,1)S(1)} collective-permute-done((bf16[640,384]{1,0:T(8,128)(2,1)S(1)}, bf16[640,384]{1,0:T(8,128)(2,1)S(1)}, u32[]{:S(2)}, u32[]{:S(2)}) %collective-permute-start.9) | collective-permute-done | bytes 491552 | tf_op jit(solution)/shard_map/ppermute | solution.py:231
  507.8 9.3 %fusion.16 = f32[1280,1792]{1,0:T(8,128)} fusion(bf16[896,1280]{1,0:T(8,128)(2,1)S(1)} %bitcast.198, bf16[896,896]{1,0:T(8,128)(2,1)} %get-tuple-element.101, bf16[896,896]{1,0:T(8,128)(2,1)} %copy-done.47), kind=kOutput, calls=%fused_computation.43 | convolution fusion | flops 4116840448 | bytes 14680064 | tf_op jit(solution)/shard_map/dot_general | solution.py:35
  517.1 3.0 slice.186
  522.3 3.9 dynamic-slice_convert_fusion
  529.1 9.7 %all-to-all-start.3 = ((bf16[16,128,384]{1,2,0:T(8,128)(2,1)}), bf16[16,128,384]{1,2,0:T(8,128)(2,1)}, u32[]{:S(2)}, u32[]{:S(2)}) async-start(bf16[16,128,384]{1,2,0:T(8,128)(2,1)} %pad_maximum_fusion.3), calls=%async_computation.5 | async-start | bytes 3145728 | tf_op jit(solution)/shard_map/all_to_all | solution.py:300
  539.7 4.9 fusion.93
  550.1 55.3 %collective-permute-done.16 = bf16[448,1280]{1,0:T(8,128)(2,1)} collective-permute-done((bf16[448,1280]{1,0:T(8,128)(2,1)S(1)}, bf16[448,1280]{1,0:T(8,128)(2,1)}, u32[]{:S(2)}, u32[]{:S(2)}) %collective-permute-start.16) | collective-permute-done | bytes 1146912 | tf_op jit(solution)/shard_map/ppermute | solution.py:231
  605.4 3.6 add_bitcast_fusion.1
  611.6 5.6 add_bitcast_fusion
  620.1 3.8 copy.158
  623.9 6.1 reshape.293
  629.9 5.7 copy.150
  642.6 33.0 %collective-permute-done.7 = bf16[640,1280]{1,0:T(8,128)(2,1)} collective-permute-done((bf16[640,1280]{1,0:T(8,128)(2,1)S(1)}, bf16[640,1280]{1,0:T(8,128)(2,1)}, u32[]{:S(2)}, u32[]{:S(2)}) %collective-permute-start.7) | collective-permute-done | bytes 1638432 | tf_op jit(solution)/shard_map/ppermute | solution.py:231
  680.8 28.2 %collective-permute-done.6 = bf16[640,1280]{1,0:T(8,128)(2,1)} collective-permute-done((bf16[640,1280]{1,0:T(8,128)(2,1)}, bf16[640,1280]{1,0:T(8,128)(2,1)}, u32[]{:S(2)}, u32[]{:S(2)}) %collective-permute-start.6) | collective-permute-done | bytes 1638432 | tf_op jit(solution)/shard_map/ppermute | solution.py:231
  721.7 5.1 slice.182
  726.8 13.3 %reshape.282 = bf16[10,640,3,128]{3,2,1,0:T(4,128)(2,1)} reshape(bf16[6400,384]{1,0:T(8,128)(2,1)} %slice.182) | data formatting | bytes 9830400 | tf_op jit(solution)/shard_map/reshape | solution.py:443
  740.1 14.6 %slice_convert_fusion.2 = (f32[10,640,1,128]{3,2,1,0:T(1,128)}, f32[10,640,1,128]{3,2,1,0:T(1,128)}, f32[10,640,1,128]{3,2,1,0:T(1,128)}) fusion(bf16[10,640,3,128]{3,2,1,0:T(4,128)(2,1)} %reshape.282), kind=kLoop, calls=%fused_computation.26 | loop fusion | flops 2457600 | bytes 14745600 | tf_op jit(solution)/shard_map/convert_element_type | solution.py:445
  754.7 4.5 copy.144
  759.3 4.5 copy.142
  763.8 4.6 copy.140
  768.4 4.6 copy.147
  772.9 4.6 copy.148
  777.5 4.7 copy.149
  782.2 5.8 add_reduce_fusion
  (274 shorter events, 114.4 us)
Async XLA Ops:
  7.2 126.8 %copy-start = (bf16[448,1280]{1,0:T(8,128)(2,1)S(1)}, bf16[448,1280]{1,0:T(8,128)(2,1)}, u32[]{:S(2)}) copy-start(bf16[448,1280]{1,0:T(8,128)(2,1)} %param.28) | copy-start | bytes 3440644
  7.2 61.8 %all-gather.19.cloned.1.call-start = ((), (), s32[]{:S(2)}) async-start(), calls=%async_computation.10 | async-start | bytes 5570560 | tf_op jit(solution)/shard_map/all_gather | solution.py:244
  7.9 159.4 %all-gather.21.cloned.1.call-start = ((), (), s32[]{:S(2)}) async-start(), calls=%async_computation.11 | async-start | bytes 5570560 | tf_op jit(solution)/shard_map/all_gather | solution.py:244
  8.7 187.9 %all-gather.15.cloned.1.call-start = ((), (), s32[]{:S(2)}) async-start(), calls=%async_computation.6 | async-start | bytes 5570560 | tf_op jit(solution)/shard_map/all_gather | solution.py:244
  11.6 7.7 copy-start.3
  11.6 7.7 copy-start.38
  11.6 7.7 copy-start.42
  11.6 9.6 %copy-start.37 = (bf16[640,16]{0,1:T(8,128)(2,1)S(1)}, bf16[640,16]{0,1:T(8,128)(2,1)}, u32[]{:S(2)}) copy-start(bf16[640,16]{0,1:T(8,128)(2,1)} %param.26) | copy-start | bytes 61444
  24.6 16.0 %collective-permute-start = (bf16[640,402]{0,1:T(8,128)(2,1)}, bf16[640,402]{0,1:T(8,128)(2,1)}, u32[]{:S(2)}, u32[]{:S(2)}) collective-permute-start(bf16[640,402]{0,1:T(8,128)(2,1)} %concatenate.98), channel_id=1, source_target_pairs={{0,1},{1,0},{2,3},{3,2},{4,5},{5,4},{6,7},{7,6},{8,9},{9,8},{10,11... | collective-permute-start | bytes 1543688 | tf_op jit(solution)/shard_map/ppermute | solution.py:231
  27.6 93.4 %collective-permute-start.1 = (bf16[640,1280]{1,0:T(8,128)(2,1)}, bf16[640,1280]{1,0:T(8,128)(2,1)}, u32[]{:S(2)}, u32[]{:S(2)}) collective-permute-start(bf16[640,1280]{1,0:T(8,128)(2,1)} %param.24), channel_id=1, source_target_pairs={{0,1},{1,0},{2,3},{3,2},{4,5},{5,4},{6,7},{7,6},{8,9},{9,8},{10,11... | collective-permute-start | bytes 4915208 | tf_op jit(solution)/shard_map/ppermute | solution.py:231
  125.5 9.2 %copy-start.40 = (s32[1,128,7]{1,0,2:T(1,128)S(1)}, s32[1,128,7]{1,0,2:T(1,128)}, u32[]{:S(2)}) copy-start(s32[1,128,7]{1,0,2:T(1,128)} %param.31) | copy-start | bytes 10756
  125.5 9.3 %copy-start.41 = (s32[1,1,896]{2,1,0:T(1,128)S(1)}, s32[1,1,896]{2,1,0:T(1,128)}, u32[]{:S(2)}) copy-start(s32[1,1,896]{2,1,0:T(1,128)} %param.32) | copy-start | bytes 10756
  127.2 208.4 %reduce-scatter.5.cloned.1.call-start = ((), (), s32[]{:S(2)}) async-start(), calls=%async_computation.8 | async-start | bytes 5570560 | tf_op jit(solution)/shard_map/reduce_scatter | solution.py:369
  127.3 72.8 %collective-permute-start.2 = (bf16[640,1792]{1,0:T(8,128)(2,1)}, bf16[640,1792]{1,0:T(8,128)(2,1)}, u32[]{:S(2)}, u32[]{:S(2)}) collective-permute-start(bf16[640,1792]{1,0:T(8,128)(2,1)} %bitcast.218), channel_id=1, source_target_pairs={{0,1},{1,0},{2,3},{3,2},{4,5},{5,4},{6,7},{7,6},{8,9},{9,8},{10,11... | collective-permute-start | bytes 6881288 | tf_op jit(solution)/shard_map/ppermute | solution.py:231
  128.8 85.8 %collective-permute-start.3 = (bf16[448,1280]{1,0:T(8,128)(2,1)}, bf16[448,1280]{1,0:T(8,128)(2,1)}, u32[]{:S(2)}, u32[]{:S(2)}) collective-permute-start(bf16[448,1280]{1,0:T(8,128)(2,1)} %bitcast.221), channel_id=1, source_target_pairs={{0,1},{1,0},{2,3},{3,2},{4,5},{5,4},{6,7},{7,6},{8,9},{9,8},{10,11... | collective-permute-start | bytes 3440648 | tf_op jit(solution)/shard_map/ppermute | solution.py:231
  132.6 114.3 %collective-permute-start.4 = (bf16[640,112]{1,0:T(8,128)(2,1)}, bf16[640,112]{1,0:T(8,128)(2,1)}, u32[]{:S(2)}, u32[]{:S(2)}) collective-permute-start(bf16[640,112]{1,0:T(8,128)(2,1)} %pad_maximum_fusion.9), channel_id=1, source_target_pairs={{0,1},{1,0},{2,3},{3,2},{4,5},{5,4},{6,7},{7,6},{8,9},{9,8},{10,11... | collective-permute-start | bytes 430088 | tf_op jit(solution)/shard_map/ppermute | solution.py:231
  134.0 115.9 %collective-permute-start.5 = (bf16[28,1280]{1,0:T(8,128)(2,1)S(1)}, bf16[28,1280]{1,0:T(8,128)(2,1)}, u32[]{:S(2)}, u32[]{:S(2)}) collective-permute-start(bf16[28,1280]{1,0:T(8,128)(2,1)S(1)} %constant_dynamic-slice_fusion.2), channel_id=1, source_target_pairs={{0,1},{1,0},{2,3},{3,2},{4,5},{5,4},{6,7},{7,6},{8,9},{9,8},{10,11... | collective-permute-start | bytes 215048 | tf_op jit(solution)/shard_map/ppermute | solution.py:231
  196.6 4.9 copy-start.43
  196.6 11.7 %slice-start = ((s8[5242880]{0:T(1024)(128)(4,1)}), s8[4194304]{0:T(1024)(128)(4,1)S(1)}, s32[]{:S(2)}) async-start(s8[5242880]{0:T(1024)(128)(4,1)} %bitcast.166), calls=%async_computation.16 | async-start | bytes 8388608
  201.4 6.9 slice-start.1
  208.3 5.3 copy-start.6
  214.6 6.7 copy-start.30
  224.4 9.7 %copy-start.23 = (bf16[896,1280]{1,0:T(8,128)(2,1)}, bf16[896,1280]{1,0:T(8,128)(2,1)S(1)}, u32[]{:S(2)}) copy-start(bf16[896,1280]{1,0:T(8,128)(2,1)S(1)} %fusion.10) | copy-start | bytes 6881284
  224.4 9.7 %copy-start.44 = (bf16[1,640,1792]{2,1,0:T(8,128)(2,1)S(1)}, bf16[1,640,1792]{2,1,0:T(8,128)(2,1)}, u32[]{:S(2)}) copy-start(bf16[1,640,1792]{2,1,0:T(8,128)(2,1)} %param.29) | copy-start | bytes 6881284
  224.4 22.5 %slice-start.2 = ((s8[5242880]{0:T(1024)(128)(4,1)}), s8[4194304]{0:T(1024)(128)(4,1)S(1)}, s32[]{:S(2)}) async-start(s8[5242880]{0:T(1024)(128)(4,1)} %bitcast.168), calls=%async_computation.18 | async-start | bytes 8388608
  224.4 25.5 %slice-start.6 = ((s8[5242880]{0:T(1024)(128)(4,1)}), s8[4194304]{0:T(1024)(128)(4,1)S(1)}, s32[]{:S(2)}) async-start(s8[5242880]{0:T(1024)(128)(4,1)} %bitcast.176), calls=%async_computation.22 | async-start | bytes 8388608
  234.1 9.3 %copy-start.47 = (bf16[896,896]{1,0:T(8,128)(2,1)}, bf16[896,896]{1,0:T(8,128)(2,1)S(1)}, u32[]{:S(2)}) copy-start(bf16[896,896]{1,0:T(8,128)(2,1)S(1)} %get-tuple-element.100) | copy-start | bytes 4816900
  234.1 12.8 %slice-start.3 = ((s8[5242880]{0:T(1024)(128)(4,1)}), s8[1048576]{0:T(1024)(128)(4,1)S(1)}, s32[]{:S(2)}) async-start(s8[5242880]{0:T(1024)(128)(4,1)} %bitcast.168), calls=%async_computation.19 | async-start | bytes 2097152
  234.1 15.8 %slice-start.7 = ((s8[5242880]{0:T(1024)(128)(4,1)}), s8[1048576]{0:T(1024)(128)(4,1)S(1)}, s32[]{:S(2)}) async-start(s8[5242880]{0:T(1024)(128)(4,1)} %bitcast.176), calls=%async_computation.23 | async-start | bytes 2097152
  252.6 5.8 copy-start.34
  252.6 9.1 %copy-start.36 = (bf16[2048,56]{0,1:T(8,128)(2,1)}, bf16[2048,56]{0,1:T(8,128)(2,1)S(1)}, u32[]{:S(2)}) copy-start(bf16[2048,56]{0,1:T(8,128)(2,1)S(1)} %get-tuple-element.128) | copy-start | bytes 688132
  258.4 158.4 %reduce-scatter.3.cloned.1.call-start = ((), (), s32[]{:S(2)}) async-start(), calls=%async_computation.7 | async-start | bytes 5570560 | tf_op jit(solution)/shard_map/reduce_scatter | solution.py:459
  266.3 69.4 %copy-start.8 = (f32[128,1280]{1,0:T(8,128)S(1)}, f32[128,1280]{1,0:T(8,128)}, u32[]{:S(2)}) copy-start(f32[128,1280]{1,0:T(8,128)} %copy-done.7) | copy-start | bytes 1966084
  266.3 9.9 %all-to-all-start.1 = ((f32[16,1,128]{2,1,0:T(1,128)}), f32[16,1,128]{2,1,0:T(1,128)S(1)}, u32[]{:S(2)}, u32[]{:S(2)}) async-start(f32[16,1,128]{2,1,0:T(1,128)} %bitcast.24), calls=%async_computation.3 | async-start | bytes 16384 | tf_op jit(solution)/shard_map/all_to_all | solution.py:353
  270.0 247.1 %all-gather.17.cloned.1.call-start = ((), (), s32[]{:S(2)}) async-start(), calls=%async_computation.9 | async-start | bytes 6893568 | tf_op jit(solution)/shard_map/all_gather | solution.py:244
  420.2 9.0 %copy-start.33 = (bf16[2048,56]{0,1:T(8,128)(2,1)S(1)}, bf16[2048,56]{0,1:T(8,128)(2,1)}, u32[]{:S(2)}) copy-start(bf16[2048,56]{0,1:T(8,128)(2,1)} %copy-done.32) | copy-start | bytes 688132
  420.2 9.0 %copy-start.35 = (bf16[2048,56]{0,1:T(8,128)(2,1)S(1)}, bf16[2048,56]{0,1:T(8,128)(2,1)}, u32[]{:S(2)}) copy-start(bf16[2048,56]{0,1:T(8,128)(2,1)} %copy-done.34) | copy-start | bytes 688132
  420.2 188.9 %all-gather.29.cloned.1.call-start = ((), (), s32[]{:S(2)}) async-start(), calls=%async_computation.15 | async-start | bytes 1392640 | tf_op jit(solution)/shard_map/all_gather | solution.py:244
  424.0 4.5 collective-permute-start.14
  437.4 30.7 %copy-start.11 = (f32[2048,128]{1,0:T(8,128)S(1)}, f32[2048,128]{1,0:T(8,128)}, u32[]{:S(2)}) copy-start(f32[2048,128]{1,0:T(8,128)} %get-tuple-element.42) | copy-start | bytes 3145732
  441.2 24.8 %all-to-all-start.2 = ((bf16[16,128,128]{1,2,0:T(8,128)(2,1)}), bf16[16,128,128]{1,2,0:T(8,128)(2,1)}, u32[]{:S(2)}, u32[]{:S(2)}) async-start(bf16[16,128,128]{1,2,0:T(8,128)(2,1)} %pad.13), calls=%async_computation.4 | async-start | bytes 1048576 | tf_op jit(solution)/shard_map/all_to_all | solution.py:393
  445.5 171.7 %all-gather.27.cloned.1.call-start = ((), (), s32[]{:S(2)}) async-start(), calls=%async_computation.14 | async-start | bytes 2437120 | tf_op jit(solution)/shard_map/all_gather | solution.py:244
  446.5 6.0 collective-permute-start.13
  454.2 267.5 %all-gather.23.cloned.1.call-start = ((), (), s32[]{:S(2)}) async-start(), calls=%async_computation.12 | async-start | bytes 8355840 | tf_op jit(solution)/shard_map/all_gather | solution.py:244
  493.5 14.3 %copy-start.25 = (bf16[16,56,1280]{2,1,0:T(8,128)(2,1)S(1)}, bf16[16,56,1280]{2,1,0:T(8,128)(2,1)}, u32[]{:S(2)}) copy-start(bf16[16,56,1280]{2,1,0:T(8,128)(2,1)} %copy-done.24) | copy-start | bytes 6881284
  493.6 13.3 %collective-permute-start.9 = (bf16[640,384]{1,0:T(8,128)(2,1)S(1)}, bf16[640,384]{1,0:T(8,128)(2,1)S(1)}, u32[]{:S(2)}, u32[]{:S(2)}) collective-permute-start(bf16[640,384]{1,0:T(8,128)(2,1)S(1)} %dynamic-slice_convert_fusion.2), channel_id=1, source_target_pairs={{0,1},{1,0},{2,3},{3,2},{4,5},{5,4},{6,7},{7,6},{8,9},{9,8},{10,11... | collective-permute-start | bytes 1474568 | tf_op jit(solution)/shard_map/ppermute | solution.py:231
  520.9 6.0 copy-start.27
  520.9 6.3 copy-start.29
  521.0 17.9 %collective-permute-start.10 = (bf16[128,1280]{1,0:T(8,128)(2,1)S(1)}, bf16[128,1280]{1,0:T(8,128)(2,1)S(1)}, u32[]{:S(2)}, u32[]{:S(2)}) collective-permute-start(bf16[128,1280]{1,0:T(8,128)(2,1)S(1)} %convolution_convert_fusion.3), channel_id=1, source_target_pairs={{0,1},{1,0},{2,3},{3,2},{4,5},{5,4},{6,7},{7,6},{8,9},{9,8},{10,11... | collective-permute-start | bytes 983048 | tf_op jit(solution)/shard_map/ppermute | solution.py:231
  526.2 85.4 %collective-permute-start.15 = (bf16[640,1792]{1,0:T(8,128)(2,1)}, bf16[640,1792]{1,0:T(8,128)(2,1)}, u32[]{:S(2)}, u32[]{:S(2)}) collective-permute-start(bf16[640,1792]{1,0:T(8,128)(2,1)} %dynamic-slice_convert_fusion), channel_id=1, source_target_pairs={{0,1},{1,0},{2,3},{3,2},{4,5},{5,4},{6,7},{7,6},{8,9},{9,8},{10,11... | collective-permute-start | bytes 6881288 | tf_op jit(solution)/shard_map/ppermute | solution.py:231
  529.1 106.5 %all-to-all-start.3 = ((bf16[16,128,384]{1,2,0:T(8,128)(2,1)}), bf16[16,128,384]{1,2,0:T(8,128)(2,1)}, u32[]{:S(2)}, u32[]{:S(2)}) async-start(bf16[16,128,384]{1,2,0:T(8,128)(2,1)} %pad_maximum_fusion.3), calls=%async_computation.5 | async-start | bytes 3145728 | tf_op jit(solution)/shard_map/all_to_all | solution.py:300
  538.8 249.8 %all-gather.25.cloned.1.call-start = ((), (), s32[]{:S(2)}) async-start(), calls=%async_computation.13 | async-start | bytes 5570560 | tf_op jit(solution)/shard_map/all_gather | solution.py:244
  539.7 8.4 %copy-start.5 = (bf16[640,1280]{1,0:T(8,128)(2,1)S(1)}, bf16[640,1280]{1,0:T(8,128)(2,1)}, u32[]{:S(2)}) copy-start(bf16[640,1280]{1,0:T(8,128)(2,1)} %param.22) | copy-start | bytes 4915204
  544.7 60.7 %collective-permute-start.16 = (bf16[448,1280]{1,0:T(8,128)(2,1)S(1)}, bf16[448,1280]{1,0:T(8,128)(2,1)}, u32[]{:S(2)}, u32[]{:S(2)}) collective-permute-start(bf16[448,1280]{1,0:T(8,128)(2,1)S(1)} %dynamic-slice_convert_fusion.1), channel_id=1, source_target_pairs={{0,1},{1,0},{2,3},{3,2},{4,5},{5,4},{6,7},{7,6},{8,9},{9,8},{10,11... | collective-permute-start | bytes 3440648 | tf_op jit(solution)/shard_map/ppermute | solution.py:231
  546.7 93.8 %collective-permute-start.8 = (bf16[640,1280]{1,0:T(8,128)(2,1)}, bf16[640,1280]{1,0:T(8,128)(2,1)}, u32[]{:S(2)}, u32[]{:S(2)}) collective-permute-start(bf16[640,1280]{1,0:T(8,128)(2,1)} %param.23), channel_id=1, source_target_pairs={{0,1},{1,0},{2,3},{3,2},{4,5},{5,4},{6,7},{7,6},{8,9},{9,8},{10,11... | collective-permute-start | bytes 4915208 | tf_op jit(solution)/shard_map/ppermute | solution.py:231
  548.1 127.6 %collective-permute-start.7 = (bf16[640,1280]{1,0:T(8,128)(2,1)S(1)}, bf16[640,1280]{1,0:T(8,128)(2,1)}, u32[]{:S(2)}, u32[]{:S(2)}) collective-permute-start(bf16[640,1280]{1,0:T(8,128)(2,1)S(1)} %copy-done.5), channel_id=1, source_target_pairs={{0,1},{1,0},{2,3},{3,2},{4,5},{5,4},{6,7},{7,6},{8,9},{9,8},{10,11... | collective-permute-start | bytes 4915208 | tf_op jit(solution)/shard_map/ppermute | solution.py:231
  548.8 160.2 %collective-permute-start.6 = (bf16[640,1280]{1,0:T(8,128)(2,1)}, bf16[640,1280]{1,0:T(8,128)(2,1)}, u32[]{:S(2)}, u32[]{:S(2)}) collective-permute-start(bf16[640,1280]{1,0:T(8,128)(2,1)} %param.21), channel_id=1, source_target_pairs={{0,1},{1,0},{2,3},{3,2},{4,5},{5,4},{6,7},{7,6},{8,9},{9,8},{10,11... | collective-permute-start | bytes 4915208 | tf_op jit(solution)/shard_map/ppermute | solution.py:231
  675.6 40.5 %slice-start.4 = ((s8[5242880]{0:T(1024)(128)(4,1)}), s8[4194304]{0:T(1024)(128)(4,1)S(1)}, s32[]{:S(2)}) async-start(s8[5242880]{0:T(1024)(128)(4,1)} %bitcast.170), calls=%async_computation.20 | async-start | bytes 8388608
  678.6 32.6 %copy-start.14 = (bf16[1,128,1280]{2,1,0:T(8,128)(2,1)S(1)}, bf16[1,128,1280]{2,1,0:T(8,128)(2,1)}, u32[]{:S(2)}) copy-start(bf16[1,128,1280]{2,1,0:T(8,128)(2,1)} %param.19) | copy-start | bytes 983044
  678.6 32.8 %copy-start.21 = (f32[128,1280]{1,0:T(8,128)S(1)}, f32[128,1280]{1,0:T(8,128)}, u32[]{:S(2)}) copy-start(f32[128,1280]{1,0:T(8,128)} %get-tuple-element.95) | copy-start | bytes 1966084
  678.6 37.6 %slice-start.5 = ((s8[5242880]{0:T(1024)(128)(4,1)}), s8[1048576]{0:T(1024)(128)(4,1)S(1)}, s32[]{:S(2)}) async-start(s8[5242880]{0:T(1024)(128)(4,1)} %bitcast.170), calls=%async_computation.21 | async-start | bytes 2097152
  714.8 3.6 collective-permute-start.11
  717.0 4.1 collective-permute-start.12
  782.2 5.8 copy-start.39
  (24 other events, 60.9 us)
Sparse Core Ops, SparseCore 0:
  10.3 58.6 all-gather.18
  71.3 63.6 all-gather.20
  137.8 58.6 all-gather.14
  258.5 77.1 reduce-scatter.4
  339.4 77.3 reduce-scatter.2
  420.3 68.2 all-gather.16
  490.8 37.7 all-gather.28
  530.8 55.6 all-gather.26
  588.8 70.0 all-gather.22
  661.0 54.3 all-gather.24

commit v2 on v1

v2 whole, which is shorter than its diff:
```python
import functools
import math

import jax
import jax.numpy as jnp
from jax import lax
from jax.experimental import pallas as pl
from jax.experimental.layout import Layout, with_layout_constraint
from jax.experimental.pallas import tpu as pltpu
from jax.sharding import PartitionSpec as P

HEADS = 10
HEAD_DIM = 128
EXP_HID = 896
TOP = 7
BLOCK = 256
TILE = 512

epsilon = 1e-06
masked_score = -1000000000.0
score_scale = 1.0 / math.sqrt(HEAD_DIM)
exact = lax.Precision.HIGHEST
f32 = jnp.float32
bf16 = jnp.bfloat16


def dot(a, b):
    return jnp.dot(a, b, preferred_element_type=f32)


def dot_nt(a, b):
    return lax.dot_general(a, b, (((1,), (1,)), ((), ())), preferred_element_type=f32)


def dot_tn(a, b):
    return lax.dot_general(a, b, (((0,), (0,)), ((), ())), preferred_element_type=f32)


def rms_scale(values):
    return lax.rsqrt(jnp.mean(values * values, axis=-1, keepdims=True) + epsilon)


def rotary_tables(positions, width):
    half = width // 2
    freqs = jnp.exp(-math.log(10000.0) * jnp.arange(half, dtype=f32) * 2.0 / width)
    angles = positions.astype(f32)[:, None] * freqs[None, :]
    cosine = jnp.concatenate([jnp.cos(angles), jnp.cos(angles)], axis=-1)
    sine = jnp.concatenate([jnp.sin(angles), jnp.sin(angles)], axis=-1)
    return (cosine, sine)


def allowed_tile(rows, columns):
    key_block = lax.broadcasted_iota(jnp.int32, (rows, columns), 0) // BLOCK
    query_block = lax.broadcasted_iota(jnp.int32, (rows, columns), 1) // BLOCK
    return key_block <= query_block


def ring_of(spans):
    if spans != 16:
        return list(range(spans))
    chips = [0, 2, 4, 6, 7, 5, 3, 1]
    return [2 * chip + core for chip in chips for core in (0, 1)]


def pieces(j, tile, length, ring):
    if ring:
        starts = (j * BLOCK, length - BLOCK - j * BLOCK)
        return [pl.ds(pl.multiple_of(at, BLOCK), BLOCK) for at in starts]
    return [pl.ds(pl.multiple_of(j * tile, tile), tile)]


def load(ref, windows, columns=slice(None)):
    parts = [ref[window, columns] for window in windows]
    return parts[0] if len(parts) == 1 else jnp.concatenate(parts, axis=0)


def store(ref, windows, value, columns=slice(None)):
    size = value.shape[0] // len(windows)
    for i, window in enumerate(windows):
        ref[window, columns] = value[i * size : (i + 1) * size]


def attend_kernel(
    ring, q_ref, k_ref, v_ref, context_ref, lse_ref, low_ref, low_ring_ref, score_ref
):
    length = k_ref.shape[0]
    tile = context_ref.shape[0]
    here = pl.program_id(0)
    queries = load(q_ref, pieces(here, tile, length, ring))

    def raw_scores(j):
        return dot_nt(load(k_ref, pieces(j, tile, length, ring)), queries) * score_scale

    def fold(j, scores, peak):
        score_ref[pl.ds(pl.multiple_of(j * tile, tile), tile), :] = scores
        return jnp.maximum(peak, jnp.max(scores.reshape(tile // 8, 8, tile), axis=0))

    diagonal = jnp.where(allowed_tile(tile, tile), raw_scores(here), masked_score)
    peak = fold(here, diagonal, jnp.full((8, tile), masked_score, f32))
    peak = lax.fori_loop(0, here, lambda j, p: fold(j, raw_scores(j), p), peak)
    top = jnp.max(peak, axis=0, keepdims=True)

    def gather(j, carry):
        total, numer = carry
        weights = jnp.exp(score_ref[pl.ds(pl.multiple_of(j * tile, tile), tile), :] - top)
        total = total + jnp.sum(weights.reshape(tile // 8, 8, tile), axis=0)
        values = load(v_ref, pieces(j, tile, length, ring))
        return total, numer + dot_tn(values, weights.astype(bf16))

    zero = (jnp.zeros((8, tile), f32), jnp.zeros((HEAD_DIM, tile), f32))
    total, numer = lax.fori_loop(0, here + 1, gather, zero)
    total = jnp.sum(total, axis=0, keepdims=True)
    context = (numer / total).T
    context_ref[...] = context
    low_ref[...] = context.astype(bf16)
    store(low_ring_ref, pieces(here, tile, length, ring), context.astype(bf16))
    lse_ref[...] = top + jnp.log(total)


def attend(query, key, value, ring):
    length = query.shape[0]
    tile = min(TILE, length)
    whole = pl.BlockSpec((length, HEAD_DIM), lambda i: (0, 0))
    part = pl.BlockSpec((tile, HEAD_DIM), lambda i: (i, 0))
    return pl.pallas_call(
        functools.partial(attend_kernel, ring),
        grid=(length // tile,),
        in_specs=[whole] * 3,
        out_specs=[part, pl.BlockSpec((1, tile), lambda i: (0, i)), part, whole],
        out_shape=[
            jax.ShapeDtypeStruct((length, HEAD_DIM), f32),
            jax.ShapeDtypeStruct((1, length), f32),
            jax.ShapeDtypeStruct((length, HEAD_DIM), bf16),
            jax.ShapeDtypeStruct((length, HEAD_DIM), bf16),
        ],
        scratch_shapes=[pltpu.VMEM((length, tile), f32)],
        name="attend",
        cost_estimate=pl.CostEstimate(
            flops=2 * length * length * HEAD_DIM,
            bytes_accessed=12 * length * HEAD_DIM,
            transcendentals=length * length // 2,
        ),
    )(query, key, value)


def attend_back_kernel(
    ring,
    q_ref,
    k_ref,
    v_ref,
    grad_ref,
    context_ref,
    lse_ref,
    cos_ref,
    sin_ref,
    out_ref,
    out_ring_ref,
    dq_ref,
    delta_ref,
    dk_ref,
    dv_ref,
):
    length = q_ref.shape[0]
    tile = dk_ref.shape[0]
    steps = length // tile
    here = pl.program_id(0)

    def natural(i):
        return pl.ds(pl.multiple_of(i * tile, tile), tile)

    @pl.when(here == 0)
    def _():
        def prepare(i, carry):
            window = natural(i)
            dq_ref[window, :] = jnp.zeros((tile, HEAD_DIM), f32)
            product = grad_ref[window, :].astype(f32) * context_ref[window, :]
            ones = jnp.ones((8, HEAD_DIM), f32)
            delta = lax.dot_general(
                ones, product, (((1,), (1,)), ((), ())), precision=exact, preferred_element_type=f32
            )
            delta_ref[:, window] = delta
            return carry

        lax.fori_loop(0, steps, prepare, 0)

    keys = load(k_ref, pieces(here, tile, length, ring))
    values = load(v_ref, pieces(here, tile, length, ring))

    def visit(i, masked):
        window = natural(i)
        queries = load(q_ref, pieces(i, tile, length, ring))
        grads = grad_ref[window, :]
        weights = jnp.exp(dot_nt(keys, queries) * score_scale - lse_ref[:, window])
        if masked:
            weights = jnp.where(allowed_tile(tile, tile), weights, 0.0)
        grad_weights = dot_nt(values, grads)
        grad_raw = (weights * (grad_weights - delta_ref[0:1, window]) * score_scale).astype(bf16)
        dq_ref[window, :] += dot_tn(grad_raw, keys)
        return dot(grad_raw, queries), dot(weights.astype(bf16), grads)

    dk, dv = visit(here, True)
    dk_ref[...] = dk
    dv_ref[...] = dv

    def step(i, carry):
        more_k, more_v = visit(i, False)
        dk_ref[...] += more_k
        dv_ref[...] += more_v
        return carry

    lax.fori_loop(here + 1, steps, step, 0)

    def write(i, part, value):
        at = slice(part * HEAD_DIM, (part + 1) * HEAD_DIM)
        out_ref[natural(i), at] = value
        store(out_ring_ref, pieces(i, tile, length, ring), value, at)

    def turned_back(i, value):
        windows = pieces(i, tile, length, ring)
        scaled = pltpu.roll(value * load(sin_ref, windows), HEAD_DIM // 2, 1)
        return (value * load(cos_ref, windows) + scaled).astype(bf16)

    write(here, 1, turned_back(here, dk_ref[...]))
    write(here, 2, dv_ref[...].astype(bf16))

    @pl.when(here == steps - 1)
    def _():
        def finish(i, carry):
            write(i, 0, turned_back(i, dq_ref[natural(i), :]))
            return carry

        lax.fori_loop(0, steps, finish, 0)


def attend_back(query, key, value, grad, context, lse, cosine, sine, ring):
    length = query.shape[0]
    tile = min(TILE, length)
    memory = pl.BlockSpec(memory_space=pltpu.VMEM)
    return pl.pallas_call(
        functools.partial(attend_back_kernel, ring),
        grid=(length // tile,),
        in_specs=[memory] * 8,
        out_specs=[memory] * 2,
        out_shape=[jax.ShapeDtypeStruct((length, 3 * HEAD_DIM), bf16)] * 2,
        scratch_shapes=[
            pltpu.VMEM((length, HEAD_DIM), f32),
            pltpu.VMEM((8, length), f32),
            pltpu.VMEM((tile, HEAD_DIM), f32),
            pltpu.VMEM((tile, HEAD_DIM), f32),
        ],
        name="attend_back",
        cost_estimate=pl.CostEstimate(
            flops=5 * length * length * HEAD_DIM,
            bytes_accessed=20 * length * HEAD_DIM,
            transcendentals=length * length // 2,
        ),
    )(query, key, value, grad, context, lse, cosine, sine)


def head_pairs(side, count):
    first = side * count
    return [(first + i, count - first + i, slice(i * HEAD_DIM, (i + 1) * HEAD_DIM)) for i in range(count)]


def mix_kernel(side_ref, got_ref, own_ref, other_ref, x_ref, gain_ref, second_ref, low_ref, scale_ref):
    second = x_ref[...].astype(f32)
    for mine, theirs, at in head_pairs(side_ref[0], HEADS // 2):
        attended = jnp.concatenate([got_ref[mine], got_ref[theirs]], axis=1)
        weight = jnp.concatenate([own_ref[at, :], other_ref[at, :]], axis=0)
        second += dot(attended, weight)
    scale = rms_scale(second)
    second_ref[...] = second
    scale_ref[...] = scale
    low_ref[...] = (second * scale * gain_ref[...]).astype(bf16)


def mix(side, got, own, other, x, gain):
    smem = pl.BlockSpec(memory_space=pltpu.SMEM)
    memory = pl.BlockSpec(memory_space=pltpu.VMEM)
    return pl.pallas_call(
        mix_kernel,
        in_specs=[smem] + [memory] * 5,
        out_specs=[memory] * 3,
        out_shape=[
            jax.ShapeDtypeStruct(x.shape, f32),
            jax.ShapeDtypeStruct(x.shape, bf16),
            jax.ShapeDtypeStruct((x.shape[0], 1), f32),
        ],
        name="mix",
    )(side.reshape(1), got, own, other, x, gain)


def mix_back_kernel(
    side_ref,
    sums_ref,
    gates_ref,
    gate_grads_ref,
    router_ref,
    second_ref,
    scale_ref,
    gain_ref,
    g_ref,
    own_ref,
    other_ref,
    carried_ref,
    grad_second_ref,
    context_ref,
    out_ref,
):
    tokens, width = second_ref.shape
    second = second_ref[...]
    scale = scale_ref[...]
    gain = gain_ref[...]
    gates = gates_ref[...]
    gate_grads = gate_grads_ref[...]
    out_ref[...] = (second + sums_ref[:, width:].astype(f32)).astype(bf16)
    weighted = gates * gate_grads
    grad_sel = weighted - gates * jnp.sum(weighted, axis=-1, keepdims=True)
    grad_logits = grad_sel.astype(bf16)
    grad_normed = sums_ref[:, :width].astype(f32) + dot_nt(grad_logits, router_ref[...])
    gain_part = jnp.sum(grad_normed * second * scale, axis=0, keepdims=True)
    hat = grad_normed * gain
    mean = jnp.mean(hat * second, axis=-1, keepdims=True)
    grad_second = g_ref[...].astype(f32) + scale * hat - second * (scale * scale * scale) * mean
    grad_second_ref[...] = grad_second
    grad_mixed = grad_second.astype(bf16)
    carried_ref[:tokens, :width] = grad_mixed
    carried_ref[:tokens, width:] = grad_logits
    high = gain_part.astype(bf16)
    rest = (gain_part - high.astype(f32)).astype(bf16)
    spare = carried_ref.shape[0] - tokens
    row = lax.broadcasted_iota(jnp.int32, (spare, width), 0)
    packed = jnp.where(row == 0, high.astype(f32), jnp.where(row == 1, rest.astype(f32), 0.0))
    carried_ref[tokens:, :width] = packed.astype(bf16)
    carried_ref[tokens:, width:] = jnp.zeros((spare, HEAD_DIM), bf16)
    for mine, theirs, at in head_pairs(side_ref[0], HEADS // 2):
        weight = jnp.concatenate([own_ref[at, :], other_ref[at, :]], axis=0)
        grad_context = dot_nt(grad_mixed, weight).astype(bf16)
        context_ref[mine] = grad_context[:, :HEAD_DIM]
        context_ref[theirs] = grad_context[:, HEAD_DIM:]
    for h in range(HEADS, context_ref.shape[0]):
        context_ref[h] = jnp.zeros((tokens, HEAD_DIM), bf16)


def mix_back(side, sums, gates, gate_grads, router, second, scale, gain, g, own, other, spans):
    tokens, width = second.shape
    smem = pl.BlockSpec(memory_space=pltpu.SMEM)
    memory = pl.BlockSpec(memory_space=pltpu.VMEM)
    return pl.pallas_call(
        mix_back_kernel,
        in_specs=[smem] + [memory] * 10,
        out_specs=[memory] * 4,
        out_shape=[
            jax.ShapeDtypeStruct((tokens + 16, width + HEAD_DIM), bf16),
            jax.ShapeDtypeStruct((tokens, width), f32),
            jax.ShapeDtypeStruct((spans, tokens, HEAD_DIM), bf16),
            jax.ShapeDtypeStruct((tokens, width), bf16),
        ],
        name="mix_back",
    )(side.reshape(1), sums, gates, gate_grads, router, second, scale, gain, g, own, other)


def inputs_back_kernel(
    side_ref,
    core_ref,
    got_ref,
    wq_ref,
    wk_ref,
    wv_ref,
    near_ref,
    far_ref,
    x_ref,
    gain_ref,
    grad_second_ref,
    out_ref,
):
    tokens, width = x_ref.shape
    half = width // 2
    count = HEADS // 2
    own_part = jnp.zeros((tokens, half), f32)
    other_part = jnp.zeros((tokens, half), f32)
    first = core_ref[0] * count
    for i, weight in enumerate((wq_ref, wk_ref, wv_ref)):
        at = slice(i * HEAD_DIM, (i + 1) * HEAD_DIM)
        for h in range(0, HEADS, 2):
            grads = jnp.concatenate([got_ref[h, :, at], got_ref[h + 1, :, at]], axis=1)
            own_part += dot_nt(grads, weight[:, h * HEAD_DIM : (h + 2) * HEAD_DIM])
        rows = slice(i * half, (i + 1) * half)
        for h in range(count):
            window = slice(h * HEAD_DIM, (h + 1) * HEAD_DIM)
            grads = jnp.concatenate(
                [got_ref[first + h, :, at], got_ref[count - first + h, :, at]], axis=1
            )
            weights = jnp.concatenate([near_ref[rows, window], far_ref[rows, window]], axis=1)
            other_part += dot_nt(grads, weights)
    grad_normed = jnp.where(
        side_ref[0] == 0,
        jnp.concatenate([own_part, other_part], axis=1),
        jnp.concatenate([other_part, own_part], axis=1),
    )
    resid = x_ref[...].astype(f32)
    scale = rms_scale(resid)
    hat = grad_normed * gain_ref[...]
    mean = jnp.mean(hat * resid, axis=-1, keepdims=True)
    out_ref[...] = grad_second_ref[...] + scale * hat - resid * (scale * scale * scale) * mean


def inputs_back(side, core, got, w_query, w_key, w_value, near, far, x, gain, grad_second):
    smem = pl.BlockSpec(memory_space=pltpu.SMEM)
    memory = pl.BlockSpec(memory_space=pltpu.VMEM)
    return pl.pallas_call(
        inputs_back_kernel,
        in_specs=[smem] * 2 + [memory] * 9,
        out_specs=memory,
        out_shape=jax.ShapeDtypeStruct(x.shape, f32),
        name="inputs_back",
    )(
        side.reshape(1),
        core.reshape(1),
        got,
        w_query,
        w_key,
        w_value,
        near,
        far,
        x,
        gain,
        grad_second,
    )


def place_heads_kernel(got_ref, wq_ref, wk_ref, wv_ref, gain_ref, q_ref, k_ref, v_ref, n_ref, sum_ref):
    here = pl.program_id(0)

    @pl.when(here == 0)
    def _():
        sum_ref[...] = jnp.zeros_like(sum_ref)

    start = got_ref.shape[2] - 3 * HEAD_DIM
    for i, (weight, out) in enumerate(((wq_ref, q_ref), (wk_ref, k_ref), (wv_ref, v_ref))):
        at = start + i * HEAD_DIM
        grad = got_ref[0, :, at : at + HEAD_DIM].astype(f32)
        out[...] = grad
        sum_ref[...] += grad * weight[...].astype(f32)

    @pl.when(here == pl.num_programs(0) - 1)
    def _():
        n_ref[...] = jnp.sum(sum_ref[...], axis=1, keepdims=True) / gain_ref[...]


def ring_position(index, spans):
    if spans != 16:
        return index
    chip, core = index // 2, index % 2
    level, column = chip // 2, chip % 2
    return (level + column * (7 - 2 * level)) * 2 + core


def place_heads(got, w_query, w_key, w_value, gain):
    spans, half, packed = got.shape
    part = pl.BlockSpec((half, HEAD_DIM), lambda h: (0, h))
    column = pl.BlockSpec((half, 1), lambda h: (0, 0))
    return pl.pallas_call(
        place_heads_kernel,
        grid=(HEADS,),
        in_specs=[
            pl.BlockSpec((1, half, packed), lambda h: (ring_position(h, spans), 0, 0)),
            part,
            part,
            part,
            column,
        ],
        out_specs=[part, part, part, column],
        out_shape=[jax.ShapeDtypeStruct(w_query.shape, f32)] * 3
        + [jax.ShapeDtypeStruct((half, 1), f32)],
        scratch_shapes=[pltpu.VMEM((half, HEAD_DIM), f32)],
        name="place_heads",
    )(got, w_query, w_key, w_value, gain)


def place_output_kernel(side_ref, got_ref, out_ref):
    wide = got_ref.shape[2]
    for block in range(out_ref.shape[1] // wide):
        rows = got_ref[0, block * HEAD_DIM : (block + 1) * HEAD_DIM, :]
        out_ref[:, block * wide : (block + 1) * wide] = rows.astype(f32)


def place_output(got, side, width):
    spans, half = got.shape[:2]
    wide = HEAD_DIM * width // half
    heads = HEADS // 2
    return pl.pallas_call(
        place_output_kernel,
        grid_spec=pltpu.PrefetchScalarGridSpec(
            num_scalar_prefetch=1,
            grid=(heads,),
            in_specs=[
                pl.BlockSpec(
                    (1, half, wide), lambda h, s: (ring_position(s[0] * heads + h, spans), 0, 0)
                )
            ],
            out_specs=pl.BlockSpec((HEAD_DIM, width), lambda h, s: (h, 0)),
        ),
        out_shape=jax.ShapeDtypeStruct((heads * HEAD_DIM, width), f32),
        name="place_output",
    )(side.reshape(1), got)


def place_shared_kernel(side_ref, got_ref, in_ref, out_ref, rows_ref):
    spans = got_ref.shape[0]
    units = got_ref.shape[1] // 4
    half = got_ref.shape[2]
    hidden = spans * units
    for part in range(2):
        for c in range(spans):
            piece = got_ref[ring_position(c, spans), part * units : (part + 1) * units, :]
            rows_ref[c * units : (c + 1) * units, :] = piece.astype(f32)
        for at in range(0, hidden, HEAD_DIM):
            in_ref[:, part * hidden + at : part * hidden + at + HEAD_DIM] = rows_ref[
                at : at + HEAD_DIM, :
            ].T
    first = side_ref[0] * (spans // 2)
    for c in range(spans // 2):
        for part in range(2):
            spot = ring_position(first + c, spans)
            piece = got_ref[spot, (2 + part) * units : (3 + part) * units, :]
            out_ref[c * units : (c + 1) * units, part * half : (part + 1) * half] = piece.astype(f32)


def place_shared(got, side):
    spans, quad, half = got.shape
    hidden = spans * quad // 4
    memory = pl.BlockSpec(memory_space=pltpu.VMEM)
    return pl.pallas_call(
        place_shared_kernel,
        in_specs=[pl.BlockSpec(memory_space=pltpu.SMEM), memory],
        out_specs=[memory, memory],
        out_shape=[
            jax.ShapeDtypeStruct((half, 2 * hidden), f32),
            jax.ShapeDtypeStruct((hidden // 2, 2 * half), f32),
        ],
        scratch_shapes=[pltpu.VMEM((hidden, half), f32)],
        name="place_shared",
    )(side.reshape(1), got)


def after(value, *others):
    return lax.optimization_barrier((value, *others))[0]


def tied(*values):
    return lax.optimization_barrier(values)


def swiglu_back(grad_hidden, gate_part, up_part):
    sigmoid = jax.nn.sigmoid(gate_part)
    grad_gate = grad_hidden * up_part * sigmoid * (1.0 + gate_part * (1.0 - sigmoid))
    grad_up = grad_hidden * jax.nn.silu(gate_part)
    return grad_gate.astype(bf16), grad_up.astype(bf16)


def slot_table(span_picks, span_order, experts):
    tokens = span_picks.shape[0]
    order = span_order.reshape(tokens, TOP)
    onehot = span_picks[:, :, None] == jnp.arange(experts, dtype=jnp.int32)
    picked = jnp.any(onehot, axis=1)
    rank_key = jnp.sum(jnp.where(onehot, order[:, :, None], 0), axis=1)
    rank_key = jnp.where(picked, rank_key, tokens * TOP)
    before = rank_key[:, None, :] < rank_key[None, :, :]
    slots = jnp.sum(before.astype(jnp.int32), axis=0)
    return jnp.where(picked, slots, tokens * TOP)


def on_device(
    inputs,
    norm1_gain,
    w_query,
    w_key,
    w_value,
    w_output,
    norm2_gain,
    router,
    shared_gate_up_weight,
    shared_down_weight,
    expert_in,
    expert_out,
    picks,
    fill_order,
    grad_out,
):
    spans = lax.axis_size("ctx")
    here = lax.axis_index("ctx")
    side = lax.axis_index("fsdp")
    core = here % 2
    tokens, width = inputs.shape[1:]
    half = width // 2
    length = spans * tokens
    experts = spans * expert_in.shape[0]
    capacity = tokens * TOP // experts
    head = jnp.minimum(here, HEADS - 1)
    units = EXP_HID // spans
    ring = ring_of(spans)
    is_ring = spans == 16
    groups = [ring] if is_ring else None
    swap_core = [(i, i ^ 1) for i in range(spans)]

    def across(value):
        return lax.ppermute(value, "fsdp", [(0, 1), (1, 0)])

    def ordered(own, other, axis):
        return jnp.where(
            side == 0,
            jnp.concatenate([own, other], axis=axis),
            jnp.concatenate([other, own], axis=axis),
        )

    def everyone(value):
        return lax.all_gather(value, "ctx", axis=0, tiled=True, axis_index_groups=groups)

    def columns(value, start, count):
        return lax.dynamic_slice_in_dim(value, start, count, 1)

    def rows(value, start, count):
        return lax.dynamic_slice_in_dim(value, start, count, 0)

    def halves(value, axis=0):
        size = value.shape[axis] // 2
        mine = lax.dynamic_slice_in_dim(value, side * size, size, axis)
        theirs = lax.dynamic_slice_in_dim(value, (1 - side) * size, size, axis)
        return mine, theirs

    def reduced(value, axis=0):
        mine, theirs = halves(value, axis)
        return mine + across(theirs.astype(bf16)).astype(f32)

    def swapped(value):
        return lax.all_to_all(value, "ctx", split_axis=0, concat_axis=0, tiled=True)

    def row_major(value):
        return with_layout_constraint(value, Layout(tuple(range(value.ndim))))

    x = inputs[0]
    g = grad_out[0]
    x_all = everyone(x)
    table = everyone(slot_table(picks[0], fill_order[0, 0], experts))
    head_parts = [columns(w, head * HEAD_DIM, HEAD_DIM) for w in (w_query, w_key, w_value)]
    small = jnp.concatenate(
        head_parts + [router, norm1_gain[:, None], norm2_gain[:, None]], axis=1
    )
    small_other = across(small)
    output_other = across(w_output)
    shared_in_own = jnp.concatenate(
        [columns(shared_gate_up_weight, at + here * units, units) for at in (0, EXP_HID)], axis=1
    )
    shared_rows = shared_down_weight.shape[0]
    shared_out_own = rows(shared_down_weight, here * units % shared_rows, units)
    ring_blocks = jnp.asarray(ring, jnp.int32)[:, None] * tokens
    positions = (ring_blocks + jnp.arange(tokens, dtype=jnp.int32)[None, :]).reshape(length)
    cosine, sine = rotary_tables(positions, HEAD_DIM)
    lane = lax.broadcasted_iota(jnp.int32, (length, HEAD_DIM), 1)
    sine = jnp.where(lane < HEAD_DIM // 2, -sine, sine)
    x_all, table, cosine, sine, small_other, output_other = tied(
        x_all, table, cosine, sine, small_other, output_other
    )
    small = ordered(small, small_other, 0)
    head_w = small[:, : 3 * HEAD_DIM]
    router_w = small[:, 3 * HEAD_DIM : 3 * HEAD_DIM + experts]
    gain_one = small[:, 3 * HEAD_DIM + experts].astype(f32).reshape(1, width)
    gain_two = small[:, 3 * HEAD_DIM + experts + 1].astype(f32).reshape(1, width)
    g_all = everyone(after(g, x_all))
    own_gate_w, own_up_w = expert_in[0, :, :EXP_HID], expert_in[0, :, EXP_HID:]
    gate_other = across(after(own_gate_w, x_all))
    up_other = across(after(own_up_w, x_all))

    resid_all = x_all.astype(f32)
    normed1_all = (resid_all * rms_scale(resid_all) * gain_one).astype(bf16)
    projected = dot(normed1_all, head_w)

    def rotate(values):
        turned = jnp.concatenate(
            [values[:, HEAD_DIM // 2 :], values[:, : HEAD_DIM // 2]], axis=1
        )
        return (values * cosine + turned * sine).astype(bf16)

    query = rotate(projected[:, :HEAD_DIM])
    key = rotate(projected[:, HEAD_DIM : 2 * HEAD_DIM])
    value = projected[:, 2 * HEAD_DIM :].astype(bf16)
    context, lse, attended, attended_ring = attend(query, key, value, is_ring)
    attended, gate_other = tied(attended, gate_other)
    down_other = across(after(expert_out[0], attended))
    shared_in_other = across(after(shared_in_own, attended))
    shared_out_other = across(after(shared_out_own, attended))
    got = swapped(attended.reshape(spans, tokens, HEAD_DIM))
    got, up_other = tied(got, up_other)
    second, normed2, scale_two = mix(side, got, w_output, output_other, x, gain_two)
    normed2_all = everyone(normed2)
    normed2_all, down_other, shared_in_other, shared_out_other = tied(
        normed2_all, down_other, shared_in_other, shared_out_other
    )
    shared_in = ordered(shared_in_own, shared_in_other, 0)
    shared_out = jnp.where(
        here * units // shared_rows == side, shared_out_own, shared_out_other
    )
    gate_w = ordered(own_gate_w, gate_other, 0)
    up_w = ordered(own_up_w, up_other, 0)
    down_w = ordered(expert_out[0], down_other, 0)
    dense = [columns(after(w, normed2_all), core * half, half) for w in (w_query, w_key, w_value)]
    near = [across(w) for w in dense]

    shared_proj = dot(normed2_all, shared_in)
    shared_gate, shared_up = shared_proj[:, :units], shared_proj[:, units:]
    shared_hidden = (jax.nn.silu(shared_gate) * shared_up).astype(bf16)
    grad_shidden = dot_nt(g_all, shared_out)
    grad_sproj = jnp.concatenate(swiglu_back(grad_shidden, shared_gate, shared_up), axis=1)
    grad_shared_in = reduced(dot_tn(grad_sproj, normed2_all), 1).astype(bf16)
    grad_shared_out = dot_tn(shared_hidden, g_all).astype(bf16)
    grad_shared_out = grad_shared_out.astype(f32) + across(grad_shared_out).astype(f32)
    grad_shared_out = grad_shared_out.astype(bf16)
    shared_grads = jnp.concatenate(
        [grad_shared_in, grad_shared_out[:, :half], grad_shared_out[:, half:]], axis=0
    )

    logits = dot(normed2_all, router_w)
    picked = table < tokens * TOP
    peak = jnp.max(jnp.where(picked, logits, masked_score), axis=-1, keepdims=True)
    chances = jnp.where(picked, jnp.exp(logits - peak), 0.0)
    gates = chances / jnp.sum(chances, axis=-1, keepdims=True)
    expert_ids = lax.broadcasted_iota(jnp.int32, (length, experts), 1)
    own_slot = jnp.sum(jnp.where(expert_ids == here, table, 0), axis=1).reshape(spans, tokens)
    own_gate = jnp.sum(jnp.where(expert_ids == here, gates, 0.0), axis=1).reshape(spans, tokens)
    takes = own_slot[:, None, :] == jnp.arange(capacity, dtype=jnp.int32)[None, :, None]
    select = takes.astype(bf16)
    slot_gate = jnp.sum(jnp.where(takes, own_gate[:, None, :], 0.0), axis=2).reshape(-1, 1)

    def to_slots(value):
        picked_rows = jnp.einsum(
            "rst,rtd->rsd",
            select,
            value.reshape(spans, tokens, width),
            preferred_element_type=bf16,
        )
        return picked_rows.reshape(spans * capacity, width)

    def from_slots(value):
        back = jnp.einsum(
            "rst,rsd->rtd",
            select,
            value.reshape(spans, capacity, width),
            preferred_element_type=f32,
        )
        return back.reshape(length, width)

    dispatched = to_slots(normed2_all)
    grad_slots = to_slots(g_all)
    gate_e, up_e = dot(dispatched, gate_w), dot(dispatched, up_w)
    expert_hidden = (jax.nn.silu(gate_e) * up_e).astype(bf16)
    expert_hidden, shared_grads, near[0] = tied(expert_hidden, shared_grads, near[0])
    shared_grads = everyone(row_major(shared_grads)[None])
    expert_result = dot(expert_hidden, down_w).astype(bf16)
    grad_slots_f = grad_slots.astype(f32)
    grad_result = (grad_slots_f * slot_gate).astype(bf16)
    slot_dot = jnp.sum(grad_slots_f * expert_result.astype(f32), axis=1).reshape(spans, capacity)
    gate_dot = jnp.sum(jnp.where(takes, slot_dot[:, :, None], 0.0), axis=1)
    out_part = from_slots(expert_result) * own_gate.reshape(-1, 1) + dot(shared_hidden, shared_out)
    grad_ehidden = dot_nt(grad_result, down_w)
    grad_gate, grad_up = swiglu_back(grad_ehidden, gate_e, up_e)
    grad_gate, near[1] = tied(grad_gate, near[1])
    grad_dispatched = (dot_nt(grad_gate, gate_w) + dot_nt(grad_up, up_w)).astype(bf16)
    grad_part = from_slots(grad_dispatched) + dot_nt(grad_sproj, shared_in)
    parts = jnp.concatenate([grad_part.astype(bf16), out_part.astype(bf16)], axis=1)
    parts, near[2] = tied(row_major(parts), near[2])
    sums = lax.psum_scatter(
        parts, "ctx", scatter_dimension=0, tiled=True, axis_index_groups=groups
    )
    spots = [ring_position(i, spans) for i in range(spans)]
    gate_dot = jnp.concatenate([gate_dot[i : i + 1] for i in spots], axis=0)
    gate_grads = swapped(after(gate_dot, parts)[:, None, :])[:, 0, :].T

    near = jnp.concatenate(near, axis=0)
    far = lax.ppermute(near, "ctx", swap_core)
    own_down, down_theirs = halves(dot_tn(expert_hidden, grad_result))
    own_gate_grad, gate_theirs = halves(dot_tn(dispatched, grad_gate))
    own_up_grad, up_theirs = halves(dot_tn(dispatched, grad_up))
    down_theirs = across(after(down_theirs.astype(bf16), parts))
    sums, gate_theirs, up_theirs, down_theirs = tied(
        sums, gate_theirs.astype(bf16), up_theirs.astype(bf16), down_theirs
    )
    gate_theirs, up_theirs = across(gate_theirs), across(up_theirs)

    own_gates = rows(gates, ring_position(here, spans) * tokens, tokens)
    padded = ((0, 0), (0, HEAD_DIM - experts))
    carried, grad_second, grad_context, layer_out = mix_back(
        side,
        sums,
        jnp.pad(own_gates, padded),
        jnp.pad(gate_grads, padded),
        jnp.pad(router_w, padded),
        second,
        scale_two,
        gain_two,
        g,
        w_output,
        output_other,
        spans,
    )
    grad_context = swapped(grad_context).reshape(length, HEAD_DIM)
    grad_context, gate_theirs = tied(grad_context, gate_theirs)
    carried = everyone(carried).reshape(spans, tokens + 16, width + HEAD_DIM)
    grad_heads, grad_heads_ring = attend_back(
        query, key, value, grad_context, context, lse, cosine, sine, is_ring
    )
    grad_heads, grad_heads_ring, up_theirs = tied(grad_heads, grad_heads_ring, up_theirs)
    grad_mixed_all = carried[:, :tokens, :width].reshape(length, width)
    grad_logits_all = carried[:, :tokens, width : width + experts].reshape(length, experts)
    norm2_all = jnp.sum(carried[:, tokens : tokens + 2, :width].astype(f32), axis=(0, 1))
    mine, theirs = halves(norm2_all)
    grad_norm2 = mine + across(theirs)
    mine, theirs = halves(dot_tn(normed2_all, grad_logits_all))
    grad_router = mine + across(theirs)
    grad_output = dot_tn(attended_ring, grad_mixed_all).astype(bf16)
    grad_output = (grad_output.astype(f32) + across(grad_output).astype(f32)).astype(bf16)
    grad_head_w = reduced(dot_tn(normed1_all, grad_heads_ring)).astype(bf16)
    wide = HEAD_DIM * width // half
    output_blocks = [grad_output[:, i : i + wide] for i in range(0, width, wide)]
    head_grads = jnp.concatenate([jnp.concatenate(output_blocks, axis=0), grad_head_w], axis=1)
    head_grads = everyone(row_major(head_grads)[None])

    got = swapped(grad_heads.reshape(spans, tokens, 3 * HEAD_DIM))
    grad_inputs = inputs_back(
        side, core, got, w_query, w_key, w_value, near, far, x, gain_one, grad_second
    )
    grad_query, grad_key, grad_value, grad_norm1 = place_heads(
        head_grads, w_query, w_key, w_value, norm1_gain[:, None].astype(f32)
    )
    grad_output = place_output(head_grads, side, width)
    grad_expert_in = jnp.concatenate(
        [own_gate_grad + gate_theirs.astype(f32), own_up_grad + up_theirs.astype(f32)], axis=1
    )
    grad_shared_in, grad_shared_out = place_shared(shared_grads, side)
    return (
        layer_out[None],
        grad_inputs[None],
        grad_norm1[:, 0],
        grad_query,
        grad_key,
        grad_value,
        grad_output,
        grad_norm2,
        grad_router,
        grad_shared_in,
        grad_shared_out,
        grad_expert_in[None],
        (own_down + down_theirs.astype(f32))[None],
    )


def solution(mesh):
    placed = (
        P("fsdp", "ctx", None),
        P("fsdp"),
        P("fsdp", None),
        P("fsdp", None),
        P("fsdp", None),
        P("fsdp", None),
        P("fsdp"),
        P("fsdp", None),
        P("fsdp", None),
        P("fsdp", None),
        P("ctx", "fsdp", None),
        P("ctx", "fsdp", None),
        P("fsdp", "ctx", None),
        P("fsdp", "ctx", None),
        P("fsdp", "ctx", None),
    )
    return jax.shard_map(
        on_device,
        mesh=mesh,
        in_specs=placed,
        out_specs=(
            P("fsdp", "ctx", None),
            P("fsdp", "ctx", None),
            P("fsdp"),
            P("fsdp", None),
            P("fsdp", None),
            P("fsdp", None),
            P("fsdp", None),
            P("fsdp"),
            P("fsdp", None),
            P("fsdp", None),
            P("fsdp", None),
            P("ctx", "fsdp", None),
            P("ctx", "fsdp", None),
        ),
        check_vma=False,
    )
```

time: 815 us -> 532 us (0.65)
  waiting for transfers between devices: 355 us -> 183 us
  local copies, waits for them, and re-layouts: 113 us -> 62.7 us
  Pallas kernels: 23.1 us -> 68.1 us
  other arithmetic: 79 us -> 43.4 us
  matrix products: 118 us -> 82.7 us
  blocking collectives: 57.5 us -> 24.9 us
    reduce_scatter x2 -> x1, waiting for transfers between devices: 136 us -> 24.1 us  [on_device(): lax.psum_scatter(parts, 'ctx', scatter_dimension=0, tiled=True, axis_inde...]
    ppermute x17 -> x19, waiting for transfers between devices: 150 us -> 85.8 us  [across(): return lax.ppermute(value, 'fsdp', [(0, 1), (1, 0)])]
    pallas_call x2 -> x8, Pallas kernels: 23.1 us -> 68.1 us  [the longest x1 17.7 us: attend_back(): pl.pallas_call(functools.partial(attend_back_kernel, ring), grid=(length...]
    convert_element_type x13 -> x6, other arithmetic: 30.8 us -> 3.25 us  [the longest x1 1.59 us: rotate(): return (values * cosine + turned * sine).astype(bf16)]
    all_to_all x1 -> x0, blocking collectives: 26.4 us -> none  [to_tokens(): got = lax.all_to_all(sent, 'ctx', split_axis=0, concat_axis=0, tiled=True)]
    dot_general x12 -> x5, matrix products: 44.1 us -> 19.6 us  [dot_nt(): lax.dot_general(a, b, (((1,), (1,)), ((), ())), preferred_element_type=f32)]
    convert_element_type x7 -> x6, local copies, waits for them, and re-layouts: 28 us -> 4.46 us  [the longest x1 1.13 us: on_device(): gate_theirs.astype(bf16)]
    all_to_all x3 -> x4, waiting for transfers between devices: 18.1 us -> 37.4 us  [swapped(): return lax.all_to_all(value, 'ctx', split_axis=0, concat_axis=0, tiled=True)]
  transfers between devices with their start and end apart: 30 -> 31, of which waited for: 16 -> 17; matrix products, arithmetic and copies ran while one was open for 36% -> 31% of each run, Pallas kernels for 3% -> 9%
where the time goes in v2:
time: 532 us; the launch traced here: 523 us
  waiting for transfers between devices  183 us (34%)
  matrix products  82.7 us (16%)
  Pallas kernels  68.1 us (13%)
  local copies, waits for them, and re-layouts  62.7 us (12%)
  other arithmetic  43.4 us (8%)
  starting transfers between devices  42.8 us (8%)
  blocking collectives  24.9 us (5%)
  between operations  15.5 us (3%)
    ppermute x19, waiting for transfers between devices, across(): return lax.ppermute(value, 'fsdp', [(0, 1), (1, 0)])  85.8 us
    all_to_all x4, waiting for transfers between devices, swapped(): return lax.all_to_all(value, 'ctx', split_axis=0, concat_axis=0, tiled=True)  37.4 us
    all_gather x6, waiting for transfers between devices, everyone(): lax.all_gather(value, 'ctx', axis=0, tiled=True, axis_index_groups=groups)  34.2 us
    dot_general x7, matrix products, dot(): return jnp.dot(a, b, preferred_element_type=f32)  31.3 us
    all_gather x1, blocking collectives, everyone(): lax.all_gather(value, 'ctx', axis=0, tiled=True, axis_index_groups=groups)  24.9 us
    unnamed x135, local copies, waits for them, and re-layouts  24.8 us
    reduce_scatter x1, waiting for transfers between devices, on_device(): lax.psum_scatter(parts, 'ctx', scatter_dimension=0, tiled=True, axis_inde...  24.1 us
    dot_general x8, matrix products, dot_tn(): lax.dot_general(a, b, (((0,), (0,)), ((), ())), preferred_element_type=f32)  22.8 us
  transfers between devices with their start and end apart: 31, of which 17 were waited for; matrix products, arithmetic and copies ran while one was open for 31% of the time, Pallas kernels for 9%

profile of v2, /device:TPU:0, one launch (start us, length us, event | category | flops | bytes accessed | tf_op | source)
XLA Modules:
  0.0 523.0 jit_solution(16034428866110108951)
XLA Ops:
  18.4 3.0 collective-permute-start
  24.1 3.7 multiply_sine_fusion
  27.8 24.9 %all_gather.22 = s32[2048,16]{1,0:T(8,128)} all-gather(s32[128,16]{1,0:T(8,128)S(1)} %broadcast_select_fusion.3), channel_id=1, replica_groups={{0,2,8,10,16,18,24,26,28,30,20,22,12,14,4,6},{1,3,9,11,17,19,25,27,29,3..., dimensions={0}, use_global_device_ids=true | all-gather | bytes 139264 | tf_op jit(solution)/shard_map/all_gather | solution.py:618
  52.7 2.0 negate_select_fusion
  54.7 14.0 %collective-permute-done.1.other_ref = bf16[640,1280]{1,0:T(8,128)(2,1)} collective-permute-done((bf16[640,1280]{1,0:T(8,128)(2,1)S(1)}, bf16[640,1280]{1,0:T(8,128)(2,1)}, u32[]{:S(2)}, u32[]{:S(2)}) %collective-permute-start.1) | collective-permute-done | bytes 1638432 | tf_op jit(solution)/shard_map/ppermute | solution.py:608
  68.7 3.2 slice_bitcast_fusion
  72.0 2.1 copy.125
  76.1 2.1 maximum_select_fusion.3
  78.7 3.6 fusion
  82.3 3.0 fusion.11
  89.4 9.7 %attend.1 = (f32[2048,128]{1,0:T(8,128)}, f32[1,2048]{1,0:T(1,128)}, bf16[2048,128]{1,0:T(8,128)(2,1)}, bf16[2048,128]{1,0:T(8,128)(2,1)}) custom-call(bf16[2048,128]{1,0:T(8,128)(2,1)} %get-tuple-element.209.q_ref, bf16[2048,128]{1,0:T(8,128)(2,1)} %get-tuple-element.208.k_ref, bf16[2048,128]{1,0:T(8,128)(2,1)} %slice.212.v_ref), custom_call_target="tpu_custom_call" | custom-call | flops 1073741824 | bytes 3145728 | tf_op jit(solution)/shard_map/attend/pallas_call | solution.py:125
  99.1 3.5 collective-permute-done.2
  102.6 6.1 %all-to-all-start = ((bf16[16,128,128]{2,1,0:T(8,128)(2,1)}), bf16[16,128,128]{2,1,0:T(8,128)(2,1)S(1)}, u32[]{:S(2)}, u32[]{:S(2)}) async-start(bf16[16,128,128]{2,1,0:T(8,128)(2,1)} %bitcast.111), calls=%async_computation | async-start | bytes 1048576 | tf_op jit(solution)/shard_map/all_to_all | solution.py:637
  109.4 16.1 %collective-permute-done.3 = bf16[640,896]{1,0:T(8,128)(2,1)} collective-permute-done((bf16[640,896]{1,0:T(8,128)(2,1)}, bf16[640,896]{1,0:T(8,128)(2,1)}, u32[]{:S(2)}, u32[]{:S(2)}) %collective-permute-start.3) | collective-permute-done | bytes 1146912 | tf_op jit(solution)/shard_map/ppermute | solution.py:608
  126.2 3.8 mix.1
  137.6 4.8 fusion.24
  142.4 18.7 %collective-permute-done.5 = bf16[640,112]{1,0:T(8,128)(2,1)S(1)} collective-permute-done((bf16[640,112]{1,0:T(8,128)(2,1)}, bf16[640,112]{1,0:T(8,128)(2,1)S(1)}, u32[]{:S(2)}, u32[]{:S(2)}) %collective-permute-start.5) | collective-permute-done | bytes 143392 | tf_op jit(solution)/shard_map/ppermute | solution.py:608
  163.3 5.3 %all-gather.12.cloned.1.call-done = bf16[2048,1280]{1,0:T(8,128)(2,1)} async-done(((bf16[128,1280]{1,0:T(8,128)(2,1)}), bf16[2048,1280]{1,0:T(8,128)(2,1)}) %all-gather.12.cloned.1.call-update) | async-done | bytes 5242896 | tf_op jit(solution)/shard_map/all_gather | solution.py:618
  168.6 4.2 select_reduce_fusion.1
  173.6 2.1 select_reduce_fusion
  175.7 1.9 fusion.46
  177.6 2.6 multiply_convert_fusion.5
  191.4 4.4 fusion.25
  195.8 7.8 %multiply_convert_fusion = (bf16[896,896]{1,0:T(8,128)(2,1)}, f32[896,896]{1,0:T(8,128)}) fusion(f32[896,896]{1,0:T(8,128)S(1)} %fusion.25, bf16[896,1280]{1,0:T(8,128)(2,1)S(1)} %bitcast.101, bf16[640,896]{1,0:T(8,128)(2,1)} %collective-permute-done.3, bf16[640,896]{1,0:T(8,128)(2,1)S(1)} %copy-done.31, pred[]{:T(512)S(6)} %eq.64), kind=kOutput, calls=%fused_computation.18 | convolution fusion | flops 2070347776 | bytes 12615681 | tf_op jit(solution)/shard_map/dot_general | solution.py:28
  204.5 4.2 collective-permute-done.10
  208.7 6.9 %fusion.7 = (f32[896]{0:T(1024)S(1)}, bf16[896,1280]{1,0:T(8,128)(2,1)}) fusion(bf16[16,56,1280]{2,1,0:T(8,128)(2,1)S(1)} %copy-done.6, bf16[896,896]{1,0:T(8,128)(2,1)} %get-tuple-element.98, bf16[448,1280]{1,0:T(8,128)(2,1)} %collective-permute-done.4, bf16[448,1280]{1,0:T(8,128)(2,1)} %bitcast.122, pred[]{:T(512)S(6)} %eq.64), kind=kOutput, calls=%fused_computation.14 | convolution fusion | flops 2071264384 | bytes 8490497 | tf_op jit(solution)/shard_map/dot_general | solution.py:28
  219.2 6.3 %multiply_convert_fusion.2 = (bf16[896,896]{1,0:T(8,128)(2,1)S(1)}, bf16[896,896]{1,0:T(8,128)(2,1)S(1)}) fusion(f32[896,896]{1,0:T(8,128)S(1)} %copy-done.58, f32[896,896]{1,0:T(8,128)} %get-tuple-element.232, bf16[896,1280]{1,0:T(8,128)(2,1)S(1)} %fusion.6, bf16[448,1280]{1,0:T(8,128)(2,1)} %collective-permute-done.4, ...), kind=kOutput, calls=%fused_computation.20 | convolution fusion | flops 2075967488 | bytes 14221313 | tf_op jit(solution)/shard_map/dot_general | solution.py:32
  226.2 4.6 fusion.26
  230.9 4.4 add_convert_fusion
  240.5 3.1 fusion.4
  243.6 6.6 %pad_maximum_fusion = bf16[2048,2560]{1,0:T(8,128)(2,1)} fusion(bf16[2048,1280]{1,0:T(8,128)(2,1)S(1)} %fusion.4, bf16[2048,1280]{1,0:T(8,128)(2,1)S(1)} %fusion.5), kind=kLoop, calls=%fused_computation.5 | loop fusion | flops 20971520 | bytes 20971520 | tf_op jit(solution)/shard_map/concatenate | solution.py:770
  253.5 4.0 fusion.53
  257.5 2.1 copy-done.20
  262.0 4.8 all-to-all-start.1
  267.1 4.2 fusion.51
  273.9 2.8 fusion.52
  276.7 2.1 copy-done.22
  279.7 7.3 %collective-permute-done.12 = bf16[448,1280]{1,0:T(8,128)(2,1)} collective-permute-done((bf16[448,1280]{1,0:T(8,128)(2,1)}, bf16[448,1280]{1,0:T(8,128)(2,1)}, u32[]{:S(2)}, u32[]{:S(2)}) %collective-permute-start.12) | collective-permute-done | bytes 1146912 | tf_op jit(solution)/shard_map/ppermute | solution.py:608
  287.0 24.1 %reduce-scatter.2.cloned.1.call-done.sums_ref = bf16[128,2560]{1,0:T(8,128)(2,1)} async-done(((bf16[2048,2560]{1,0:T(8,128)(2,1)}), bf16[128,2560]{1,0:T(8,128)(2,1)}) %reduce-scatter.2.cloned.1.call-update) | async-done | bytes 655376 | tf_op jit(solution)/shard_map/reduce_scatter | solution.py:772
  311.1 5.2 mix_back.1
  318.5 5.2 all-to-all-start.2
  324.8 21.8 %all-to-all-done.2 = bf16[16,128,128]{2,1,0:T(8,128)(2,1)} async-done(((bf16[16,128,128]{2,1,0:T(8,128)(2,1)}), bf16[16,128,128]{2,1,0:T(8,128)(2,1)}, u32[]{:S(2)}, u32[]{:S(2)}) %all-to-all-start.2) | async-done | bytes 524320 | tf_op jit(solution)/shard_map/all_to_all | solution.py:637
  346.6 17.7 %attend_back.1 = (bf16[2048,384]{1,0:T(8,128)(2,1)}, bf16[2048,384]{1,0:T(8,128)(2,1)}) custom-call(bf16[2048,128]{1,0:T(8,128)(2,1)} %get-tuple-element.209.q_ref, bf16[2048,128]{1,0:T(8,128)(2,1)} %get-tuple-element.208.k_ref, bf16[2048,128]{1,0:T(8,128)(2,1)} %slice.212.v_ref, bf16[2048,128]{1,0:T(8,128)(2,1)} %bitcast.25.grad_ref, ...), custom_call_target="tpu_custom_call" | custom-call | flops 2684354560 | bytes 5242880 | tf_op jit(solution)/shard_map/attend_back/pallas_call | solution.py:239
  364.3 4.8 collective-permute-done.14
  369.0 5.6 %fusion.9 = f32[1280,384]{1,0:T(8,128)S(1)} fusion(bf16[2048,384]{1,0:T(8,128)(2,1)} %get-tuple-element.122, bf16[2048,1280]{1,0:T(8,128)(2,1)} %bitcast.93, f32[1280]{0:T(1024)S(1)} %get-tuple-element.199, f32[2048]{0:T(1024)S(1)} %add_rsqrt_fusion), kind=kOutput, calls=%fused_computation.37 | convolution fusion | flops 2023751680 | bytes 8795136 | tf_op jit(solution)/shard_map/dot_general | solution.py:36
  376.3 2.9 slice.171
  380.9 8.2 %collective-permute-done.17 = bf16[640,384]{1,0:T(8,128)(2,1)} collective-permute-done((bf16[640,384]{1,0:T(8,128)(2,1)S(1)}, bf16[640,384]{1,0:T(8,128)(2,1)}, u32[]{:S(2)}, u32[]{:S(2)}) %collective-permute-start.17) | collective-permute-done | bytes 491552 | tf_op jit(solution)/shard_map/ppermute | solution.py:608
  390.2 4.1 collective-permute-done.16
  395.5 5.2 all-to-all-start.3
  400.7 2.1 constant_dynamic-update-slice_fusion.2
  402.8 2.1 constant_dynamic-update-slice_fusion.1
  404.9 2.1 constant_dynamic-update-slice_fusion.near_ref
  409.0 5.9 %place_shared.1 = (f32[640,1792]{1,0:T(8,128)}, f32[448,1280]{1,0:T(8,128)}) custom-call(s32[1]{0:T(128)} %bitcast.side_ref, bf16[16,224,640]{2,1,0:T(8,128)(2,1)} %bitcast.97), custom_call_target="tpu_custom_call" | custom-call | tf_op jit(solution)/shard_map/place_shared/pallas_call | solution.py:534
  414.9 3.7 add_bitcast_fusion
  420.5 2.2 convert_add_fusion
  422.7 2.5 maximum_bitcast_fusion
  425.2 5.7 %copy.142 = f32[1,640,1792]{2,1,0:T(8,128)} copy(f32[1,640,1792]{1,2,0:T(8,128)} %maximum_bitcast_fusion) | data formatting | bytes 9175040
  430.9 15.7 %all-to-all-done.3.got_ref = bf16[16,128,384]{2,1,0:T(8,128)(2,1)S(1)} async-done(((bf16[16,128,384]{2,1,0:T(8,128)(2,1)}), bf16[16,128,384]{2,1,0:T(8,128)(2,1)S(1)}, u32[]{:S(2)}, u32[]{:S(2)}) %all-to-all-start.3) | async-done | bytes 1572896 | tf_op jit(solution)/shard_map/all_to_all | solution.py:637
  447.7 8.6 %inputs_back.1 = f32[128,1280]{1,0:T(8,128)} custom-call(s32[1]{0:T(128)} %bitcast.side_ref, s32[1]{0:T(128)} %bitcast.24.core_ref, bf16[16,128,384]{2,1,0:T(8,128)(2,1)} %copy-done.8, bf16[640,1280]{1,0:T(8,128)(2,1)} %wq_ref.3, bf16[640,1280]{1,0:T(8,128)(2,1)} %wk_ref.3, bf16[640,1280]{1,0:T(8,128)(2,1)} %wv_ref.3, ...), custom_call_target="tpu_custom_call" | custom-call | tf_op jit(solution)/shard_map/inputs_back/pallas_call | solution.py:411
  460.0 3.4 fusion.54
  464.8 2.8 collective-permute-done.19
  468.2 28.9 %all-gather.18.cloned.1.call-done = bf16[10240,640]{1,0:T(8,128)(2,1)} async-done(((bf16[640,640]{1,0:T(8,128)(2,1)}), bf16[10240,640]{1,0:T(8,128)(2,1)}) %all-gather.18.cloned.1.call-update) | async-done | bytes 13107216 | tf_op jit(solution)/shard_map/all_gather | solution.py:618
  497.1 4.4 place_output.1
  501.5 12.7 %place_heads.1 = (f32[640,1280]{1,0:T(8,128)}, f32[640,1280]{1,0:T(8,128)}, f32[640,1280]{1,0:T(8,128)}, f32[640,1]{1,0:T(8,128)}) custom-call(bf16[16,640,640]{2,1,0:T(8,128)(2,1)} %bitcast.84, bf16[640,1280]{1,0:T(8,128)(2,1)} %wq_ref.3, bf16[640,1280]{1,0:T(8,128)(2,1)} %wk_ref.3, bf16[640,1280]{1,0:T(8,128)(2,1)} %wv_ref.3, f32[640,1]{1,0:T(8,128)} %copy.141.gain_ref), custom_call_target="tpu_custom_call" | custom-call | tf_op jit(solution)/shard_map/place_heads/pallas_call | solution.py:463
  (262 shorter events, 83.8 us)
Async XLA Ops:
  7.2 127.2 %copy-start = (bf16[448,1280]{1,0:T(8,128)(2,1)S(1)}, bf16[448,1280]{1,0:T(8,128)(2,1)}, u32[]{:S(2)}) copy-start(bf16[448,1280]{1,0:T(8,128)(2,1)} %param.25) | copy-start | bytes 3440644
  7.2 14.2 %copy-start.7 = (bf16[640,1280]{1,0:T(8,128)(2,1)S(1)}, bf16[640,1280]{1,0:T(8,128)(2,1)}, u32[]{:S(2)}) copy-start(bf16[640,1280]{1,0:T(8,128)(2,1)} %own_ref.3) | copy-start | bytes 4915204
  7.2 14.2 %copy-start.50 = (s32[1,128,7]{1,0,2:T(1,128)S(1)}, s32[1,128,7]{1,0,2:T(1,128)}, u32[]{:S(2)}) copy-start(s32[1,128,7]{1,0,2:T(1,128)} %param.28) | copy-start | bytes 10756
  7.2 14.3 %copy-start.51 = (s32[1,1,896]{2,1,0:T(1,128)S(1)}, s32[1,1,896]{2,1,0:T(1,128)}, u32[]{:S(2)}) copy-start(s32[1,1,896]{2,1,0:T(1,128)} %param.29) | copy-start | bytes 10756
  7.2 61.4 %all-gather.16.cloned.1.call-start = ((), (), s32[]{:S(2)}) async-start(), calls=%async_computation.9 | async-start | bytes 5570560 | tf_op jit(solution)/shard_map/all_gather | solution.py:618
  8.0 129.6 %all-gather.10.cloned.1.call-start = ((), (), s32[]{:S(2)}) async-start(), calls=%async_computation.5 | async-start | bytes 5570560 | tf_op jit(solution)/shard_map/all_gather | solution.py:618
  11.0 13.0 %copy-start.52 = (s32[16]{0:T(128)S(1)}, s32[16]{0:T(128)}, u32[]{:S(2)}) copy-start(s32[16]{0:T(128)} %constant.129) | copy-start | bytes 196
  18.4 36.3 %collective-permute-start = (bf16[640,402]{0,1:T(8,128)(2,1)}, bf16[640,402]{0,1:T(8,128)(2,1)}, u32[]{:S(2)}, u32[]{:S(2)}) collective-permute-start(bf16[640,402]{0,1:T(8,128)(2,1)} %copy.124), channel_id=1, source_target_pairs={{0,1},{1,0},{2,3},{3,2},{4,5},{5,4},{6,7},{7,6},{8,9},{9,8},{10,11... | collective-permute-start | bytes 1543688 | tf_op jit(solution)/shard_map/ppermute | solution.py:608
  21.4 47.3 %collective-permute-start.1 = (bf16[640,1280]{1,0:T(8,128)(2,1)S(1)}, bf16[640,1280]{1,0:T(8,128)(2,1)}, u32[]{:S(2)}, u32[]{:S(2)}) collective-permute-start(bf16[640,1280]{1,0:T(8,128)(2,1)S(1)} %copy-done.7), channel_id=1, source_target_pairs={{0,1},{1,0},{2,3},{3,2},{4,5},{5,4},{6,7},{7,6},{8,9},{9,8},{10,11... | collective-permute-start | bytes 4915208 | tf_op jit(solution)/shard_map/ppermute | solution.py:608
  68.7 13.6 %slice-start.2 = ((s8[5242880]{0:T(1024)(128)(4,1)}), s8[1048576]{0:T(1024)(128)(4,1)S(1)}, s32[]{:S(2)}) async-start(s8[5242880]{0:T(1024)(128)(4,1)} %bitcast.94), calls=%async_computation.14 | async-start | bytes 2097152
  74.1 28.5 %collective-permute-start.2 = (bf16[640,896]{1,0:T(8,128)(2,1)}, bf16[640,896]{1,0:T(8,128)(2,1)}, u32[]{:S(2)}, u32[]{:S(2)}) collective-permute-start(bf16[640,896]{1,0:T(8,128)(2,1)} %get-tuple-element.80), channel_id=1, source_target_pairs={{0,1},{1,0},{2,3},{3,2},{4,5},{5,4},{6,7},{7,6},{8,9},{9,8},{10,11... | collective-permute-start | bytes 3440648 | tf_op jit(solution)/shard_map/ppermute | solution.py:608
  75.8 6.5 %slice-start.3 = ((s8[5242880]{0:T(1024)(128)(4,1)}), s8[4194304]{0:T(1024)(128)(4,1)S(1)}, s32[]{:S(2)}) async-start(s8[5242880]{0:T(1024)(128)(4,1)} %bitcast.94), calls=%async_computation.15 | async-start | bytes 8388608
  75.8 49.6 %collective-permute-start.3 = (bf16[640,896]{1,0:T(8,128)(2,1)}, bf16[640,896]{1,0:T(8,128)(2,1)}, u32[]{:S(2)}, u32[]{:S(2)}) collective-permute-start(bf16[640,896]{1,0:T(8,128)(2,1)} %get-tuple-element.82), channel_id=1, source_target_pairs={{0,1},{1,0},{2,3},{3,2},{4,5},{5,4},{6,7},{7,6},{8,9},{9,8},{10,11... | collective-permute-start | bytes 3440648 | tf_op jit(solution)/shard_map/ppermute | solution.py:608
  78.2 4.1 copy-start.12
  102.6 22.8 %all-to-all-start = ((bf16[16,128,128]{2,1,0:T(8,128)(2,1)}), bf16[16,128,128]{2,1,0:T(8,128)(2,1)S(1)}, u32[]{:S(2)}, u32[]{:S(2)}) async-start(bf16[16,128,128]{2,1,0:T(8,128)(2,1)} %bitcast.111), calls=%async_computation | async-start | bytes 1048576 | tf_op jit(solution)/shard_map/all_to_all | solution.py:637
  108.7 59.8 %all-gather.12.cloned.1.call-start = ((), (), s32[]{:S(2)}) async-start(), calls=%async_computation.6 | async-start | bytes 5570560 | tf_op jit(solution)/shard_map/all_gather | solution.py:618
  126.2 8.9 %copy-start.11 = (s32[2048,16]{1,0:T(8,128)S(1)}, s32[2048,16]{1,0:T(8,128)}, u32[]{:S(2)}) copy-start(s32[2048,16]{1,0:T(8,128)} %all_gather.22) | copy-start | bytes 393220
  130.1 181.0 %reduce-scatter.2.cloned.1.call-start = ((), (), s32[]{:S(2)}) async-start(), calls=%async_computation.7 | async-start | bytes 11141120 | tf_op jit(solution)/shard_map/reduce_scatter | solution.py:772
  130.2 32.4 %collective-permute-start.4 = (bf16[448,1280]{1,0:T(8,128)(2,1)}, bf16[448,1280]{1,0:T(8,128)(2,1)}, u32[]{:S(2)}, u32[]{:S(2)}) collective-permute-start(bf16[448,1280]{1,0:T(8,128)(2,1)} %bitcast.121), channel_id=1, source_target_pairs={{0,1},{1,0},{2,3},{3,2},{4,5},{5,4},{6,7},{7,6},{8,9},{9,8},{10,11... | collective-permute-start | bytes 3440648 | tf_op jit(solution)/shard_map/ppermute | solution.py:608
  135.5 25.6 %collective-permute-start.5 = (bf16[640,112]{1,0:T(8,128)(2,1)}, bf16[640,112]{1,0:T(8,128)(2,1)S(1)}, u32[]{:S(2)}, u32[]{:S(2)}) collective-permute-start(bf16[640,112]{1,0:T(8,128)(2,1)} %pad_maximum_fusion.7), channel_id=1, source_target_pairs={{0,1},{1,0},{2,3},{3,2},{4,5},{5,4},{6,7},{7,6},{8,9},{9,8},{10,11... | collective-permute-start | bytes 430088 | tf_op jit(solution)/shard_map/ppermute | solution.py:608
  136.1 26.5 %collective-permute-start.6 = (bf16[56,1280]{1,0:T(8,128)(2,1)}, bf16[56,1280]{1,0:T(8,128)(2,1)S(1)}, u32[]{:S(2)}, u32[]{:S(2)}) collective-permute-start(bf16[56,1280]{1,0:T(8,128)(2,1)} %constant_dynamic-slice_fusion.5), channel_id=1, source_target_pairs={{0,1},{1,0},{2,3},{3,2},{4,5},{5,4},{6,7},{7,6},{8,9},{9,8},{10,11... | collective-permute-start | bytes 430088 | tf_op jit(solution)/shard_map/ppermute | solution.py:608
  137.6 31.0 %copy-start.13 = (bf16[1280,402]{1,0:T(8,128)(2,1)S(1)}, bf16[1280,402]{1,0:T(8,128)(2,1)}, u32[]{:S(2)}) copy-start(bf16[1280,402]{1,0:T(8,128)(2,1)} %copy-done.12) | copy-start | bytes 3087364
  168.6 7.1 %copy-start.2 = (bf16[2048,1280]{1,0:T(8,128)(2,1)S(1)}, bf16[2048,1280]{1,0:T(8,128)(2,1)}, u32[]{:S(2)}) copy-start(bf16[2048,1280]{1,0:T(8,128)(2,1)} %all-gather.12.cloned.1.call-done) | copy-start | bytes 15728644
  173.6 4.0 slice-start
  181.3 22.4 %collective-permute-start.8 = (bf16[112,640]{1,0:T(8,128)(2,1)S(1)}, bf16[112,640]{1,0:T(8,128)(2,1)S(1)}, u32[]{:S(2)}, u32[]{:S(2)}) collective-permute-start(bf16[112,640]{1,0:T(8,128)(2,1)S(1)} %dynamic-slice_convert_fusion.4), channel_id=1, source_target_pairs={{0,1},{1,0},{2,3},{3,2},{4,5},{5,4},{6,7},{7,6},{8,9},{9,8},{10,11... | collective-permute-start | bytes 430088 | tf_op jit(solution)/shard_map/ppermute | solution.py:608
  182.9 20.7 %collective-permute-start.9 = (bf16[56,1280]{1,0:T(8,128)(2,1)S(1)}, bf16[56,1280]{1,0:T(8,128)(2,1)S(1)}, u32[]{:S(2)}, u32[]{:S(2)}) collective-permute-start(bf16[56,1280]{1,0:T(8,128)(2,1)S(1)} %convolution_convert_fusion.2), channel_id=1, source_target_pairs={{0,1},{1,0},{2,3},{3,2},{4,5},{5,4},{6,7},{7,6},{8,9},{9,8},{10,11... | collective-permute-start | bytes 430088 | tf_op jit(solution)/shard_map/ppermute | solution.py:608
  184.4 3.0 copy-start.5
  185.9 9.9 %copy-start.23 = (bf16[16,56,1280]{2,1,0:T(8,128)(2,1)}, bf16[16,56,1280]{2,1,0:T(8,128)(2,1)S(1)}, u32[]{:S(2)}) copy-start(bf16[16,56,1280]{2,1,0:T(8,128)(2,1)S(1)} %fusion.23) | copy-start | bytes 6881284
  185.9 4.0 copy-start.4
  185.9 5.5 %copy-start.29 = (bf16[640,896]{1,0:T(8,128)(2,1)S(1)}, bf16[640,896]{1,0:T(8,128)(2,1)}, u32[]{:S(2)}) copy-start(bf16[640,896]{1,0:T(8,128)(2,1)} %get-tuple-element.80) | copy-start | bytes 3440644
  186.8 21.8 %collective-permute-start.10 = (bf16[640,640]{1,0:T(8,128)(2,1)}, bf16[640,640]{1,0:T(8,128)(2,1)}, u32[]{:S(2)}, u32[]{:S(2)}) collective-permute-start(bf16[640,640]{1,0:T(8,128)(2,1)} %constant_dynamic-slice_fusion.3), channel_id=1, source_target_pairs={{0,1},{1,0},{2,3},{3,2},{4,5},{5,4},{6,7},{7,6},{8,9},{9,8},{10,11... | collective-permute-start | bytes 2457608 | tf_op jit(solution)/shard_map/ppermute | solution.py:608
  188.4 37.8 %collective-permute-start.7 = (bf16[640,640]{1,0:T(8,128)(2,1)}, bf16[640,640]{1,0:T(8,128)(2,1)}, u32[]{:S(2)}, u32[]{:S(2)}) collective-permute-start(bf16[640,640]{1,0:T(8,128)(2,1)} %constant_dynamic-slice_fusion.4), channel_id=1, source_target_pairs={{0,1},{1,0},{2,3},{3,2},{4,5},{5,4},{6,7},{7,6},{8,9},{9,8},{10,11... | collective-permute-start | bytes 2457608 | tf_op jit(solution)/shard_map/ppermute | solution.py:608
  190.8 59.4 %collective-permute-start.11 = (bf16[640,640]{1,0:T(8,128)(2,1)}, bf16[640,640]{1,0:T(8,128)(2,1)}, u32[]{:S(2)}, u32[]{:S(2)}) collective-permute-start(bf16[640,640]{1,0:T(8,128)(2,1)} %constant_dynamic-slice_fusion.2), channel_id=1, source_target_pairs={{0,1},{1,0},{2,3},{3,2},{4,5},{5,4},{6,7},{7,6},{8,9},{9,8},{10,11... | collective-permute-start | bytes 2457608 | tf_op jit(solution)/shard_map/ppermute | solution.py:608
  191.4 4.4 copy-start.31
  195.8 7.8 %copy-start.57 = (f32[896,896]{1,0:T(8,128)}, f32[896,896]{1,0:T(8,128)S(1)}, u32[]{:S(2)}) copy-start(f32[896,896]{1,0:T(8,128)S(1)} %fusion.25) | copy-start | bytes 9633796
  195.8 12.8 %copy-start.6 = (bf16[16,56,1280]{2,1,0:T(8,128)(2,1)S(1)}, bf16[16,56,1280]{2,1,0:T(8,128)(2,1)}, u32[]{:S(2)}) copy-start(bf16[16,56,1280]{2,1,0:T(8,128)(2,1)} %fusion.24) | copy-start | bytes 6881284
  216.1 3.1 copy-start.58
  216.6 8.9 %copy-start.25 = (bf16[896,1280]{1,0:T(8,128)(2,1)}, bf16[896,1280]{1,0:T(8,128)(2,1)S(1)}, u32[]{:S(2)}) copy-start(bf16[896,1280]{1,0:T(8,128)(2,1)S(1)} %fusion.6) | copy-start | bytes 6881284
  219.2 7.0 %copy-start.32 = (bf16[640,896]{1,0:T(8,128)(2,1)S(1)}, bf16[640,896]{1,0:T(8,128)(2,1)}, u32[]{:S(2)}) copy-start(bf16[640,896]{1,0:T(8,128)(2,1)} %get-tuple-element.82) | copy-start | bytes 3440644
  225.5 5.3 %copy-start.54 = (bf16[896,896]{1,0:T(8,128)(2,1)}, bf16[896,896]{1,0:T(8,128)(2,1)S(1)}, u32[]{:S(2)}) copy-start(bf16[896,896]{1,0:T(8,128)(2,1)S(1)} %get-tuple-element.207) | copy-start | bytes 4816900
  225.5 5.3 %copy-start.56 = (bf16[896,896]{1,0:T(8,128)(2,1)}, bf16[896,896]{1,0:T(8,128)(2,1)S(1)}, u32[]{:S(2)}) copy-start(bf16[896,896]{1,0:T(8,128)(2,1)S(1)} %get-tuple-element.94) | copy-start | bytes 4816900
  226.2 4.6 copy-start.30
  250.3 3.2 copy-start.26
  259.6 7.5 %copy-start.24 = (bf16[16,56,1280]{2,1,0:T(8,128)(2,1)S(1)}, bf16[16,56,1280]{2,1,0:T(8,128)(2,1)}, u32[]{:S(2)}) copy-start(bf16[16,56,1280]{2,1,0:T(8,128)(2,1)} %copy-done.23) | copy-start | bytes 6881284
  260.8 26.2 %collective-permute-start.12 = (bf16[448,1280]{1,0:T(8,128)(2,1)}, bf16[448,1280]{1,0:T(8,128)(2,1)}, u32[]{:S(2)}, u32[]{:S(2)}) collective-permute-start(bf16[448,1280]{1,0:T(8,128)(2,1)} %dynamic-slice_convert_fusion), channel_id=1, source_target_pairs={{0,1},{1,0},{2,3},{3,2},{4,5},{5,4},{6,7},{7,6},{8,9},{9,8},{10,11... | collective-permute-start | bytes 3440648 | tf_op jit(solution)/shard_map/ppermute | solution.py:608
  262.0 17.0 %all-to-all-start.1 = ((f32[16,1,128]{2,1,0:T(1,128)}), f32[16,1,128]{2,1,0:T(1,128)S(1)}, u32[]{:S(2)}, u32[]{:S(2)}) async-start(f32[16,1,128]{2,1,0:T(1,128)} %bitcast.20), calls=%async_computation.2 | async-start | bytes 16384 | tf_op jit(solution)/shard_map/all_to_all | solution.py:637
  266.8 109.4 %all-gather.14.cloned.1.call-start = ((), (), s32[]{:S(2)}) async-start(), calls=%async_computation.8 | async-start | bytes 6893568 | tf_op jit(solution)/shard_map/all_gather | solution.py:618
  271.3 5.4 %copy-start.21 = (f32[1280,896]{0,1:T(8,128)}, f32[1280,896]{0,1:T(8,128)S(1)}, u32[]{:S(2)}) copy-start(f32[1280,896]{0,1:T(8,128)S(1)} %fusion.51) | copy-start | bytes 13762564
  311.1 5.8 %copy-start.33 = (bf16[640,896]{0,1:T(8,128)(2,1)S(1)}, bf16[640,896]{0,1:T(8,128)(2,1)}, u32[]{:S(2)}) copy-start(bf16[640,896]{0,1:T(8,128)(2,1)} %dynamic-slice_convert_fusion.2) | copy-start | bytes 3440644
  316.3 92.7 %all-gather.20.cloned.1.call-start = ((), (), s32[]{:S(2)}) async-start(), calls=%async_computation.11 | async-start | bytes 4874240 | tf_op jit(solution)/shard_map/all_gather | solution.py:618
  316.9 29.7 %collective-permute-start.13 = (bf16[640,896]{0,1:T(8,128)(2,1)S(1)}, bf16[640,896]{0,1:T(8,128)(2,1)S(1)}, u32[]{:S(2)}, u32[]{:S(2)}) collective-permute-start(bf16[640,896]{0,1:T(8,128)(2,1)S(1)} %copy-done.33), channel_id=1, source_target_pairs={{0,1},{1,0},{2,3},{3,2},{4,5},{5,4},{6,7},{7,6},{8,9},{9,8},{10,11... | collective-permute-start | bytes 3440648 | tf_op jit(solution)/shard_map/ppermute | solution.py:608
  318.5 28.1 %all-to-all-start.2 = ((bf16[16,128,128]{2,1,0:T(8,128)(2,1)}), bf16[16,128,128]{2,1,0:T(8,128)(2,1)}, u32[]{:S(2)}, u32[]{:S(2)}) async-start(bf16[16,128,128]{2,1,0:T(8,128)(2,1)} %get-tuple-element.107), calls=%async_computation.3 | async-start | bytes 1048576 | tf_op jit(solution)/shard_map/all_to_all | solution.py:637
  323.7 173.4 %all-gather.18.cloned.1.call-start = ((), (), s32[]{:S(2)}) async-start(), calls=%async_computation.10 | async-start | bytes 13926400 | tf_op jit(solution)/shard_map/all_gather | solution.py:618
  324.2 44.8 %collective-permute-start.14 = (bf16[640,896]{0,1:T(8,128)(2,1)S(1)}, bf16[640,896]{0,1:T(8,128)(2,1)}, u32[]{:S(2)}, u32[]{:S(2)}) collective-permute-start(bf16[640,896]{0,1:T(8,128)(2,1)S(1)} %dynamic-slice_convert_fusion.1), channel_id=1, source_target_pairs={{0,1},{1,0},{2,3},{3,2},{4,5},{5,4},{6,7},{7,6},{8,9},{9,8},{10,11... | collective-permute-start | bytes 3440648 | tf_op jit(solution)/shard_map/ppermute | solution.py:608
  346.6 17.7 %copy-start.34 = (bf16[640,896]{0,1:T(8,128)(2,1)}, bf16[640,896]{0,1:T(8,128)(2,1)S(1)}, u32[]{:S(2)}) copy-start(bf16[640,896]{0,1:T(8,128)(2,1)S(1)} %collective-permute-done.13) | copy-start | bytes 3440644
  374.7 14.3 %collective-permute-start.17 = (bf16[640,384]{1,0:T(8,128)(2,1)S(1)}, bf16[640,384]{1,0:T(8,128)(2,1)}, u32[]{:S(2)}, u32[]{:S(2)}) collective-permute-start(bf16[640,384]{1,0:T(8,128)(2,1)S(1)} %dynamic-slice_convert_fusion.3), channel_id=1, source_target_pairs={{0,1},{1,0},{2,3},{3,2},{4,5},{5,4},{6,7},{7,6},{8,9},{9,8},{10,11... | collective-permute-start | bytes 1474568 | tf_op jit(solution)/shard_map/ppermute | solution.py:608
  380.1 14.2 %collective-permute-start.16 = (bf16[128,1280]{1,0:T(8,128)(2,1)S(1)}, bf16[128,1280]{1,0:T(8,128)(2,1)S(1)}, u32[]{:S(2)}, u32[]{:S(2)}) collective-permute-start(bf16[128,1280]{1,0:T(8,128)(2,1)S(1)} %convolution_convert_fusion.1), channel_id=1, source_target_pairs={{0,1},{1,0},{2,3},{3,2},{4,5},{5,4},{6,7},{7,6},{8,9},{9,8},{10,11... | collective-permute-start | bytes 983048 | tf_op jit(solution)/shard_map/ppermute | solution.py:608
  395.5 51.1 %all-to-all-start.3 = ((bf16[16,128,384]{2,1,0:T(8,128)(2,1)}), bf16[16,128,384]{2,1,0:T(8,128)(2,1)S(1)}, u32[]{:S(2)}, u32[]{:S(2)}) async-start(bf16[16,128,384]{2,1,0:T(8,128)(2,1)} %bitcast.107), calls=%async_computation.4 | async-start | bytes 3145728 | tf_op jit(solution)/shard_map/all_to_all | solution.py:637
  400.7 6.8 %copy-start.49 = (bf16[640]{0:T(1024)(128)(2,1)S(1)}, bf16[640]{0:T(1024)(128)(2,1)}, u32[]{:S(2)}) copy-start(bf16[640]{0:T(1024)(128)(2,1)} %param.17) | copy-start | bytes 3844
  407.0 23.8 %collective-permute-start.15 = (bf16[1920,640]{1,0:T(8,128)(2,1)}, bf16[1920,640]{1,0:T(8,128)(2,1)}, u32[]{:S(2)}, u32[]{:S(2)}) collective-permute-start(bf16[1920,640]{1,0:T(8,128)(2,1)} %constant_dynamic-update-slice_fusion.near_ref), channel_id=1, source_target_pairs={{0,2},{2,0},{4,6},{6,4},{8,10},{10,8},{12,14},{14,12},{16,18},{18,... | collective-permute-start | bytes 7372808 | tf_op jit(solution)/shard_map/ppermute | solution.py:780
  414.9 3.7 copy-start.35
  458.6 5.5 %collective-permute-start.18 = (f32[640]{0:T(1024)S(1)}, f32[640]{0:T(1024)S(1)}, u32[]{:S(2)}, u32[]{:S(2)}) collective-permute-start(f32[640]{0:T(1024)S(1)} %dynamic_slice.90), channel_id=1, source_target_pairs={{0,1},{1,0},{2,3},{3,2},{4,5},{5,4},{6,7},{7,6},{8,9},{9,8},{10,11... | collective-permute-start | bytes 7688 | tf_op jit(solution)/shard_map/ppermute | solution.py:608
  463.5 4.1 collective-permute-start.19
  501.5 14.4 %copy-start.1 = (bf16[448,1280]{1,0:T(8,128)(2,1)S(1)}, bf16[448,1280]{1,0:T(8,128)(2,1)}, u32[]{:S(2)}) copy-start(bf16[448,1280]{1,0:T(8,128)(2,1)} %param.25) | copy-start | bytes 3440644
  (31 other events, 52.0 us)
Sparse Core Ops, SparseCore 0:
  9.7 44.1 all-gather.15
  68.8 38.4 all-gather.9
  130.2 38.3 all-gather.11
  250.4 60.6 reduce-scatter.1
  316.4 52.2 all-gather.13
  370.2 34.8 all-gather.19
  407.3 89.7 all-gather.17
